TPU v7x, 32 devices: a whole 2x2x4 slice. The times are simulated.
32 devices in a mesh: lon: 8 (over y, x, core), lat: 4 (over z).
Axes of the slice: x: 2, y: 2, z: 4, core: 2. Of those that a mesh axis runs over, the one named last changes fastest.
Arguments:
- thermal_anomaly: float32 [12, 128, 3072], P(None, 'lat', 'lon'), may hold values from -6 to 6
- saltiness_anomaly: float32 [12, 128, 3072], P(None, 'lat', 'lon'), may hold values from -6 to 6
- zonal_current: float32 [12, 128, 3072], P(None, 'lat', 'lon'), may hold values from -1.8 to 1.8
- meridional_current: float32 [12, 128, 3072], P(None, 'lat', 'lon'), may hold values from -1.8 to 1.8
- free_elevation: float32 [128, 3072], P('lat', 'lon'), may hold values from -1.8 to 1.8
- zonal_traction: float32 [128, 3072], P('lat', 'lon'), may hold values from -6 to 6
- meridional_traction: float32 [128, 3072], P('lat', 'lon'), may hold values from -6 to 6
- water_indicator: int32 [128, 3072], P('lat', 'lon'), may hold values 0 or 1
- bottom_layer_index: int32 [128, 3072], P('lat', 'lon'), may hold values from 1 to 12
Outputs:
- temperature_next: float32 [12, 128, 3072], P(None, 'lat', 'lon')
- salinity_next: float32 [12, 128, 3072], P(None, 'lat', 'lon')
- u_next: float32 [12, 128, 3072], P(None, 'lat', 'lon')
- v_next: float32 [12, 128, 3072], P(None, 'lat', 'lon')
- height_next: float32 [128, 3072], P('lat', 'lon')
- transport_x: float32 [128, 3072], P('lat', 'lon')
- transport_y: float32 [128, 3072], P('lat', 'lon')
All inputs are finite; a program needn't handle non-finite values. No bound on the sum of `water_indicator` on one device may be relied on, other than what follows from the above.
Results may differ from a plain program's by a relative error of at most 0.00002.
Values sent between devices are 32-bit elements; how exact they have to be, the bound alone decides.
A program may use at most 64 MiB of HBM per device.

v0:
```python
import functools

import jax
import jax.numpy as jnp
from jax import lax
from jax.experimental import pallas as pl
from jax.experimental.pallas import tpu as pltpu
from jax.sharding import PartitionSpec as P

NSUB = 4
TIME_STEP = 0.4
TRACER_DIFF = 0.05
MOMENTUM_DIFF = 0.05
BOTTOM_DRAG = 0.05
WIND_FACTOR = 0.5
CORIOLIS_SCALE = 0.5
LATITUDE_SPAN = 2.6
GRAVITY_FACTOR = 0.3
THERMAL_COEF = 0.2
HALINE_COEF = 0.8
BACKGROUND_MIX = 0.05
CONVECTIVE_MIX = 1.5
STABILITY_FACTOR = 5.0
HEIGHT_FACTOR = 0.2
SLOPE_FACTOR = 0.15

LANES = 128
SUB = 8
FLAT = 6
MESH = pl.DeviceIdType.MESH
F32 = jnp.float32


def lane_of(shape):
    return lax.broadcasted_iota(jnp.int32, shape, len(shape) - 1)


def east(x, lane, s=1):
    r = pltpu.roll(x, LANES - s, 2)
    return jnp.where(lane < LANES - s, r[:-1], r[1:])


def west(x, lane):
    r = pltpu.roll(x, 1, 2)
    return jnp.where(lane >= 1, r[:-1], jnp.concatenate([r[-1:], r[:-2]], axis=0))


def east_all(x, lane, s=1):
    r = pltpu.roll(x, LANES - s, 2)
    return jnp.where(lane < LANES - s, r, jnp.concatenate([r[1:], r[:1]], axis=0))


def west_all(x, lane):
    r = pltpu.roll(x, 1, 2)
    return jnp.where(lane >= 1, r, jnp.concatenate([r[-1:], r[:-1]], axis=0))


def step_loop(first, last, unroll, body, carry):
    n = (last - first) // unroll

    def group(g, c):
        for i in range(unroll):
            c = body(first + g * unroll + i, c)
        return c

    carry = lax.fori_loop(0, n, group, carry)
    for k in range(first + n * unroll, last):
        carry = body(jnp.int32(k), carry)
    return carry


def face_weights(speed, opening):
    p = speed * (TIME_STEP / 12.0)
    q = jnp.abs(p)
    m = 3.0 * q - jnp.where(opening, TIME_STEP * TRACER_DIFF, 0.0)
    p7 = 7.0 * p
    return p7 - m, p7 + m, p + q, q - p


def kernel(
    lat_total,
    t_in, s_in, u_in, v_in, eta_in, zt_in, mt_in, wi_in, bi_in,
    t_out, s_out, u_out, v_out, flat_out,
    tr, sr, ur, vr, tm, sm, um, vm, pm, xt, xs, yt, ys, ratio,
    zt, mt, wi, bi, de, hue, hve, flat, fu_ref, fv_ref,
    strip1, fe1, fw1, strip2, fe2, fw2,
    load_sem, send1, recv1, send2, recv2,
):
    levels, nt, rows, _ = t_out.shape
    end = SUB + rows
    nr = rows // SUB
    lon, lat = lax.axis_index("lon"), lax.axis_index("lat")
    nlon, nlat = lax.axis_size("lon"), lax.axis_size("lat")
    wst, est = lax.rem(lon + nlon - 1, nlon), lax.rem(lon + 1, nlon)
    nth, sth = lax.rem(lat + 1, nlat), lax.rem(lat + nlat - 1, nlat)
    has_n, has_s = lat < nlat - 1, lat > 0
    own = pl.ds(SUB, rows)

    loads = []

    def load(src, dst):
        group = []
        for c in range(nt):
            cols = pl.ds(c * LANES, LANES)
            group.append(pltpu.make_async_copy(
                src(cols), dst(c), load_sem.at[len(loads) * nt + c]))
            group[-1].start()
        loads.append(group)
        return group

    ld_wi = load(lambda s: wi_in.at[:, s], lambda c: wi.at[c])
    ld_bi = load(lambda s: bi_in.at[:, s], lambda c: bi.at[c])
    ld_t = load(lambda s: t_in.at[:, :, s], lambda c: tr.at[:, c])
    ld_s = load(lambda s: s_in.at[:, :, s], lambda c: sr.at[:, c])
    ld_u = load(lambda s: u_in.at[:, :, s], lambda c: ur.at[:, c, own, :])
    ld_v = load(lambda s: v_in.at[:, :, s], lambda c: vr.at[:, c, own, :])
    ld_e = load(lambda s: eta_in.at[:, s], lambda c: flat.at[0, c, own, :])
    ld_z = load(lambda s: zt_in.at[:, s], lambda c: zt.at[c])
    ld_m = load(lambda s: mt_in.at[:, s], lambda c: mt.at[c])

    def arrived(*groups):
        for g in groups:
            for c in g:
                c.wait()

    de[:, 0:SUB, :] = jnp.zeros((nt + 1, SUB, LANES), F32)
    de[:, end:, :] = jnp.zeros((nt + 1, 2 * SUB, LANES), F32)
    for ref in (fe1, fw1):
        ref[:, 0:SUB, :] = jnp.zeros((2, SUB, LANES), F32)
        ref[:, end:, :] = jnp.zeros((2, SUB, LANES), F32)
    for ref in (fe2, fw2):
        ref[0:SUB, :] = jnp.zeros((SUB, LANES), F32)
        ref[end:, :] = jnp.zeros((SUB, LANES), F32)
    for f in range(FLAT):
        flat[f, :, 0:SUB, :] = jnp.zeros((nt, SUB, LANES), F32)
        flat[f, :, end:, :] = jnp.zeros((nt, SUB, LANES), F32)
    for ref in (tm, sm):
        for k in range(levels):
            ref[k, 0:nt, 0:SUB, :] = jnp.zeros((nt, SUB, LANES), F32)
            ref[k, 0:nt, end:, :] = jnp.zeros((nt, SUB, LANES), F32)

    barrier = pltpu.get_barrier_semaphore()

    def greet(lo, la):
        pl.semaphore_signal(barrier, inc=1, device_id=(lo, la), device_id_type=MESH)

    greet(wst, lat)
    greet(est, lat)

    @pl.when(has_n)
    def _():
        greet(wst, nth)
        greet(lon, nth)
        greet(est, nth)

    @pl.when(has_s)
    def _():
        greet(wst, sth)
        greet(lon, sth)
        greet(est, sth)

    def copier(send, recv):
        made = []

        def cp(src, dst, lo, la):
            n = len(made)
            made.append(pltpu.make_async_remote_copy(
                src_ref=src, dst_ref=dst, send_sem=send.at[n], recv_sem=recv.at[n],
                device_id=(lo, la), device_id_type=MESH))
            return made[-1]

        return cp

    def start_ns(up, down):
        @pl.when(has_n)
        def _():
            for c in up:
                c.start()

        @pl.when(has_s)
        def _():
            for c in down:
                c.start()

    def recv_ns(up, down):
        @pl.when(has_s)
        def _():
            for c in up:
                c.wait_recv()

        @pl.when(has_n)
        def _():
            for c in down:
                c.wait_recv()

    def sent_ns(up, down):
        @pl.when(has_n)
        def _():
            for c in up:
                c.wait_send()

        @pl.when(has_s)
        def _():
            for c in down:
                c.wait_send()

    cp = copier(send1, recv1)

    def rows_up(ref, n, at):
        return cp(at(ref, end - n, n), at(ref, SUB - n, n), lon, nth)

    def rows_down(ref, n, at):
        return cp(at(ref, SUB, n), at(ref, end, n), lon, sth)

    def cube_rows(ref, first, n):
        return ref.at[:, 0:nt, pl.ds(first, n), :]

    def plane_rows(ref, first, n):
        return ref.at[0:nt, pl.ds(first, n), :]

    depth_up, depth_down = [rows_up(de, 2, plane_rows)], [rows_down(de, 2, plane_rows)]
    flow_up = [rows_up(r, 1, cube_rows) for r in (ur, vr)]
    flow_down = [rows_down(r, 1, cube_rows) for r in (ur, vr)]
    tracer_up = [rows_up(r, 2, cube_rows) for r in (tm, sm)]
    tracer_down = [rows_down(r, 2, cube_rows) for r in (tm, sm)]

    def strips(cp, strip, fe, fw, at, n):
        along = [cp(at(strip, 0, rows), at(fe, SUB, rows), wst, lat),
                 cp(at(strip, 0, rows), at(fw, SUB, rows), est, lat)]
        up = [cp(at(strip, rows - n, n), at(fe, SUB - n, n), wst, nth),
              cp(at(strip, rows - n, n), at(fw, SUB - n, n), est, nth)]
        down = [cp(at(strip, 0, n), at(fe, end, n), wst, sth),
                cp(at(strip, 0, n), at(fw, end, n), est, sth)]
        return along, up, down

    along1, corner_up1, corner_down1 = strips(
        cp, strip1, fe1, fw1, lambda r, a, n: r.at[:, pl.ds(a, n), :], 2)

    lane = lane_of((SUB, LANES))
    tall = lane_of((rows, LANES))

    sub = lax.broadcasted_iota(jnp.int32, (SUB, LANES), 0)
    j = (lat * rows + sub + SUB * lax.rem(lane, nr)).astype(F32)
    j = j + jnp.where(lane < LANES // 2, 0.5, 1.0)
    f = CORIOLIS_SCALE * jnp.sin(LATITUDE_SPAN * (j / lat_total - 0.5)) * (0.25 * TIME_STEP)
    for r in range(nr):
        fu_ref[r] = jnp.broadcast_to(f[:, r:r + 1], (SUB, LANES))
        at = LANES // 2 - (LANES // 2) % nr + nr + r
        fv_ref[r] = jnp.broadcast_to(f[:, at:at + 1], (SUB, LANES))

    arrived(ld_wi, ld_bi)
    depth = (wi[...] * bi[...]).astype(F32)
    de[0:nt, own, :] = depth
    arrived(ld_t, ld_s, ld_u, ld_v)
    pl.semaphore_wait(barrier, 2 + 3 * has_n.astype(jnp.int32) + 3 * has_s.astype(jnp.int32))
    start_ns(depth_up, depth_down)
    start_ns(flow_up, flow_down)

    place = lax.shift_right_logical(tall, 2)

    def edge(first, last, p):
        return pltpu.roll(jnp.where(tall < LANES // 2, first, last), 4 * p + 2, 1)

    group_a = edge(depth[0], depth[nt - 1], 2 * levels)
    group_b = jnp.zeros((rows, LANES), F32)
    for k in range(levels):
        wet = de[0:nt, own, :] > k
        t = jnp.where(wet, tr[k], 0.0)
        s = jnp.where(wet, sr[k], 0.0)
        tm[k, 0:nt, own, :] = t
        sm[k, 0:nt, own, :] = s
        group_a = jnp.where(place == 2 * k, edge(t[0], t[nt - 1], 2 * k), group_a)
        group_a = jnp.where(place == 2 * k + 1, edge(s[0], s[nt - 1], 2 * k + 1), group_a)
        group_b = jnp.where(place == 2 * k, edge(ur[k, 0, own, :], ur[k, nt - 1, own, :], 2 * k), group_b)
        group_b = jnp.where(place == 2 * k + 1, edge(vr[k, 0, own, :], vr[k, nt - 1, own, :], 2 * k + 1), group_b)
    strip1[0] = group_a
    strip1[1] = group_b
    for c in along1:
        c.start()
    start_ns(corner_up1, corner_down1)
    start_ns(tracer_up, tracer_down)

    HALF = 0.5 * GRAVITY_FACTOR * TIME_STEP

    def pressure(t, s, total):
        h = (HALF * HALINE_COEF) * s - (HALF * THERMAL_COEF) * t
        p = total + h
        return p, p + h

    def own_pressure(k, total):
        p, total = pressure(tm[k, 0:nt, own, :], sm[k, 0:nt, own, :], total)
        pm[k, 0:nt, own, :] = p
        return total

    lax.fori_loop(0, levels, own_pressure, jnp.zeros((nt, rows, LANES), F32))
    arrived(ld_e, ld_z, ld_m)
    flat[5, :, own, :] = depth

    for c in along1:
        c.wait_recv()
    recv_ns(corner_up1, corner_down1)
    recv_ns(depth_up, depth_down)

    pair = (lane_of((end + SUB, LANES)) & 3) >= 2
    halo_a = jnp.where(pair, fe1[0], fw1[0])
    halo_b = jnp.where(pair, fe1[1], fw1[1])
    fe1[0] = halo_a
    fe1[1] = halo_b
    de[nt, 0:end + SUB, :] = pltpu.roll(halo_a, LANES - (8 * levels + 2), 1)
    for r in range(0, end + SUB, SUB):
        d = de[:, r:r + SUB, :]
        hue[:, r:r + SUB, :] = jnp.minimum(d, east_all(d, lane))
        hve[:, r:r + SUB, :] = jnp.minimum(d, de[:, r + 1:r + SUB + 1, :])

    def edges(k, total):
        kf = k.astype(F32)
        back = LANES - 2 - 8 * k
        a = fe1[0, own, :]
        t = pltpu.roll(a, back, 1)
        s = pltpu.roll(a, back - 4, 1)
        tm[k, nt, own, :] = t
        sm[k, nt, own, :] = s
        p, total = pressure(t, s, total)
        pm[k, nt, own, :] = p
        b = fe1[1]
        um[k, nt] = jnp.where(hue[nt] > kf, pltpu.roll(b, back, 1), 0.0)
        vm[k, nt] = jnp.where(hve[nt] > kf, pltpu.roll(b, back - 4, 1), 0.0)
        um[k, 0:nt, own, :] = jnp.where(hue[0:nt, own, :] > kf, ur[k, :, own, :], 0.0)
        vm[k, 0:nt, own, :] = jnp.where(hve[0:nt, own, :] > kf, vr[k, :, own, :], 0.0)
        return total

    total = jnp.zeros((rows, LANES), F32)
    for k in range(levels):
        total = edges(jnp.int32(k), total)

    @pl.loop(0, levels)
    def _(k):
        kf = k.astype(F32)
        for r in range(SUB, end, SUB):
            here = slice(r, r + SUB)
            w0, w1, w2, w3 = face_weights(um[k, :, here, :], hue[:, here, :] > kf)
            for ref, to in ((tm, xt), (sm, xs)):
                c = ref[k, :, here, :]
                fx = (w0 * c + w1 * east_all(c, lane)
                      - w2 * east_all(c, lane, 2) + w3 * west_all(c, lane))
                to[k, :, r - SUB:r, :] = c[:nt] - (fx[:nt] - west(fx, lane))

    recv_ns(flow_up, flow_down)
    recv_ns(tracer_up, tracer_down)

    def far_rows(k, total):
        kf = k.astype(F32)
        for a in (0, end):
            out = slice(a, a + SUB)
            um[k, 0:nt, out, :] = jnp.where(hue[0:nt, out, :] > kf, ur[k, :, out, :], 0.0)
            vm[k, 0:nt, out, :] = jnp.where(hve[0:nt, out, :] > kf, vr[k, :, out, :], 0.0)
        out = slice(end, end + SUB)
        p, total = pressure(tm[k, 0:nt, out, :], sm[k, 0:nt, out, :], total)
        pm[k, 0:nt, out, :] = p
        return total

    step_loop(0, levels, 2, far_rows, jnp.zeros((nt, SUB, LANES), F32))

    MIX = TIME_STEP * MOMENTUM_DIFF
    KEEP = 1.0 - TIME_STEP * BOTTOM_DRAG - 4.0 * MIX
    for r in range(nr):
        at = SUB + SUB * r
        here, above, below = slice(at, at + SUB), slice(at + 1, at + SUB + 1), slice(at - 1, at + SUB - 1)
        out = slice(SUB * r, SUB * r + SUB)

        def momentum(k, carry, wind=None):
            su, sv, tu, tv = carry
            kf = k.astype(F32)
            u4, un = um[k, :, here, :], um[k, :, above, :]
            v4, vs = vm[k, :, here, :], vm[k, :, below, :]
            u, v = u4[:nt], v4[:nt]
            around_u = east(u4, lane) + west(u4, lane) + un[:nt] + um[k, 0:nt, below, :]
            around_v = east(v4, lane) + west(v4, lane) + vs[:nt] + vm[k, 0:nt, above, :]
            a, b = v4 + vs, u4 + un
            vbar = a[:nt] + east(a, lane)
            ubar = b[:nt] + west(b, lane)
            p = pm[k, :, here, :]
            px = east(p, lane) - p[:nt]
            py = pm[k, 0:nt, above, :] - p[:nt]
            ut = KEEP * u + MIX * around_u + fu_ref[r] * vbar - px
            vt = KEEP * v + MIX * around_v - fv_ref[r] * ubar - py
            if wind is not None:
                ut = ut + wind * zt[:, out, :]
                vt = vt + wind * mt[:, out, :]
            ut = jnp.where(hue[0:nt, here, :] > kf, ut, 0.0)
            vt = jnp.where(hve[0:nt, here, :] > kf, vt, 0.0)
            u_out[k, :, out, :] = ut
            v_out[k, :, out, :] = vt
            return su + u, sv + v, tu + ut, tv + vt

        zero = jnp.zeros((nt, SUB, LANES), F32)
        carry = momentum(jnp.int32(0), (zero,) * 4, TIME_STEP * WIND_FACTOR)
        su, sv, tu, tv = step_loop(1, levels, 2, momentum, carry)
        flat[1, :, here, :] = su
        flat[2, :, here, :] = sv
        flat[3, :, here, :] = tu - su
        flat[4, :, here, :] = tv - sv

    spot = lax.shift_right_logical(tall, 3)
    group = jnp.zeros((rows, LANES), F32)
    for f in range(FLAT):
        x = jnp.where(tall < LANES // 2, flat[f, 0, own, :], flat[f, nt - 1, own, :])
        group = jnp.where(spot == f, pltpu.roll(x, 8 * f + 4, 1), group)
    strip2[...] = group
    cp = copier(send2, recv2)
    flat_up = [cp(cube_rows(flat, end - NSUB, NSUB), cube_rows(flat, SUB - NSUB, NSUB), lon, nth)]
    flat_down = [cp(cube_rows(flat, SUB, NSUB), cube_rows(flat, end, NSUB), lon, sth)]
    along2, corner_up2, corner_down2 = strips(
        cp, strip2, fe2, fw2, lambda r, a, n: r.at[pl.ds(a, n), :], NSUB)
    start_ns(flat_up, flat_down)
    for c in along2:
        c.start()
    start_ns(corner_up2, corner_down2)

    starts = list(range(SUB - 1, end - SUB, SUB)) + [end - SUB]

    @pl.loop(0, levels)
    def _(k):
        kf = k.astype(F32)
        for a in starts:
            here = slice(a, a + SUB)
            w0, w1, w2, w3 = face_weights(vm[k, 0:nt, here, :], hve[0:nt, here, :] > kf)
            for ref, to in ((tm, yt), (sm, ys)):
                to[k, :, here, :] = (
                    w0 * ref[k, 0:nt, here, :] + w1 * ref[k, 0:nt, a + 1:a + SUB + 1, :]
                    - w2 * ref[k, 0:nt, a + 2:a + SUB + 2, :] + w3 * ref[k, 0:nt, a - 1:a + SUB - 1, :])

    span = 2 * SUB if rows % (2 * SUB) == 0 else SUB
    DIFF = TIME_STEP * STABILITY_FACTOR * BACKGROUND_MIX
    BASE = TIME_STEP * (BACKGROUND_MIX + CONVECTIVE_MIX)
    for r in range(0, rows, span):
        out = slice(r, r + span)
        here, below = slice(SUB + r, SUB + r + span), slice(SUB + r - 1, SUB + r + span - 1)

        def star(k):
            t = xt[k, :, out, :] - (yt[k, :, here, :] - yt[k, :, below, :])
            s = xs[k, :, out, :] - (ys[k, :, here, :] - ys[k, :, below, :])
            return t, s, HALINE_COEF * s - THERMAL_COEF * t

        def forward(k, carry):
            t, s, dens, lower, qt, qs = carry
            tn, sn, densn = star(k)
            rise = jnp.maximum(densn - dens, 0.0)
            e = 1.0 + STABILITY_FACTOR * rise
            n = jnp.where(de[0:nt, here, :] > k.astype(F32), BASE + DIFF * rise, 0.0)
            w = 1.0 / (e * lower + n)
            rat = n * w
            ew = e * w
            gt, gs = t + qt, s + qs
            t_out[k - 1, :, out, :] = gt * ew
            s_out[k - 1, :, out, :] = gs * ew
            ratio[k - 1, :, out, :] = rat
            return tn, sn, densn, 1.0 + rat * lower, rat * gt, rat * gs

        zero = jnp.zeros((nt, span, LANES), F32)
        carry = star(0) + (zero + 1.0, zero, zero)
        t, s, _, lower, qt, qs = lax.fori_loop(1, levels, forward, carry)
        w = 1.0 / lower
        t, s = (t + qt) * w, (s + qs) * w
        t_out[levels - 1, :, out, :] = t
        s_out[levels - 1, :, out, :] = s

        def backward(i, carry):
            t, s = carry
            k = levels - 2 - i
            rat = ratio[k, :, out, :]
            t = t_out[k, :, out, :] + rat * t
            s = s_out[k, :, out, :] + rat * s
            t_out[k, :, out, :] = t
            s_out[k, :, out, :] = s
            return t, s

        lax.fori_loop(0, levels - 1, backward, (t, s))

    recv_ns(flat_up, flat_down)
    for c in along2:
        c.wait_recv()
    recv_ns(corner_up2, corner_down2)
    wide = slice(SUB - NSUB, end + NSUB)
    count = rows + 2 * NSUB
    halo = jnp.where((lane_of((count, LANES)) & 7) >= 4, fe2[wide, :], fw2[wide, :])
    for f in range(FLAT):
        flat_out[f, 0:nt, 0:count] = flat[f, :, wide, :]
        flat_out[f, nt, 0:count] = pltpu.roll(halo, LANES - 8 * f - 4, 1)
    flat_out[5, :, count:, :] = jnp.zeros((nt + 1, SUB, LANES), F32)

    for c in along1 + along2:
        c.wait_send()
    sent_ns(depth_up + flow_up + tracer_up + corner_up1 + flat_up + corner_up2,
            depth_down + flow_down + tracer_down + corner_down1 + flat_down + corner_down2)


def tail(
    t, s, ut, vt, flat,
    t_out, s_out, u_out, v_out, eta_out, tx_out, ty_out,
    eta, bu, bv, hx, hy, un, vn, cor, sem,
):
    levels, nt, rows, _ = t.shape
    count = rows + 2 * NSUB
    lane = lane_of((SUB, LANES))
    copies = []

    def put(src, dst):
        for c in range(nt):
            copies.append(pltpu.make_async_copy(
                src(c), dst(pl.ds(c * LANES, LANES)), sem.at[len(copies)]))
            copies[-1].start()

    put(lambda c: t.at[:, c], lambda d: t_out.at[:, :, d])
    put(lambda c: s.at[:, c], lambda d: s_out.at[:, :, d])

    for ref in (eta, bu, bv):
        ref[:, 0:SUB, :] = jnp.zeros((nt + 1, SUB, LANES), F32)
        ref[:, count + SUB:, :] = jnp.zeros((nt + 1, SUB, LANES), F32)
    tiles = range(0, count, SUB)
    eta[:, SUB:count + SUB, :] = flat[0, :, 0:count, :]
    bu[:, SUB:count + SUB, :] = flat[1, :, 0:count, :]
    bv[:, SUB:count + SUB, :] = flat[2, :, 0:count, :]
    for r in tiles:
        d = flat[5, :, r:r + SUB, :]
        hx[:, r:r + SUB, :] = jnp.minimum(d, east_all(d, lane))
        hy[:, r:r + SUB, :] = jnp.minimum(d, flat[5, :, r + 1:r + SUB + 1, :])
    for sub in range(NSUB):
        for r in tiles:
            here, below = slice(SUB + r, 2 * SUB + r), slice(SUB + r - 1, 2 * SUB + r - 1)
            x = bu[:, here, :]
            eta[:, here, :] = eta[:, here, :] - HEIGHT_FACTOR * (
                x - west_all(x, lane) + (bv[:, here, :] - bv[:, below, :]))
        for r in tiles:
            here, above = slice(SUB + r, 2 * SUB + r), slice(SUB + r + 1, 2 * SUB + r + 1)
            raw = slice(r, r + SUB)
            x = eta[:, here, :]
            bu[:, here, :] = (bu[:, here, :] + (1.0 / NSUB) * flat[3, :, raw, :]
                              - SLOPE_FACTOR * hx[:, raw, :] * (east_all(x, lane) - x))
            bv[:, here, :] = (bv[:, here, :] + (1.0 / NSUB) * flat[4, :, raw, :]
                              - SLOPE_FACTOR * hy[:, raw, :] * (eta[:, above, :] - x))
    mid = pl.ds(SUB + NSUB, rows)
    put(lambda c: eta.at[c, mid, :], lambda d: eta_out.at[:, d])
    put(lambda c: bu.at[c, mid, :], lambda d: tx_out.at[:, d])
    put(lambda c: bv.at[c, mid, :], lambda d: ty_out.at[:, d])

    for r in range(0, rows, SUB):
        raw = slice(NSUB + r, NSUB + r + SUB)
        hu, hv = hx[0:nt, raw, :], hy[0:nt, raw, :]
        done = slice(SUB + NSUB + r, 2 * SUB + NSUB + r)
        out = slice(r, r + SUB)
        cor[0, :, out, :] = (bu[0:nt, done, :] - (flat[3, 0:nt, raw, :] + flat[1, 0:nt, raw, :])) / jnp.maximum(hu, 1.0)
        cor[1, :, out, :] = (bv[0:nt, done, :] - (flat[4, 0:nt, raw, :] + flat[2, 0:nt, raw, :])) / jnp.maximum(hv, 1.0)
        cor[2, :, out, :] = hu
        cor[3, :, out, :] = hv

    @pl.loop(0, levels)
    def _(k):
        kf = k.astype(F32)
        un[k] = jnp.where(cor[2] > kf, ut[k] + cor[0], 0.0)
        vn[k] = jnp.where(cor[3] > kf, vt[k] + cor[1], 0.0)

    put(lambda c: un.at[:, c], lambda d: u_out.at[:, :, d])
    put(lambda c: vn.at[:, c], lambda d: v_out.at[:, :, d])
    for c in copies:
        c.wait()


def body(*args):
    levels, rows, cols = args[0].shape
    nt = cols // LANES
    erows = rows + 2 * SUB
    count = rows + 2 * NSUB

    def vmem(*shape):
        return pltpu.VMEM(shape, F32)

    def out(*shape):
        return jax.ShapeDtypeStruct(shape, F32)

    block = pl.BlockSpec(memory_space=pltpu.VMEM)
    far = pl.BlockSpec(memory_space=pltpu.HBM)
    raw = vmem(levels, nt, erows, LANES)
    own = vmem(levels, nt, rows, LANES)
    wide = vmem(levels, nt + 1, erows, LANES)
    ints = pltpu.VMEM((nt, rows, LANES), jnp.int32)
    n1, n2 = 2 + 4 + 4 + 6, 2 + 6
    cube = (levels, nt, rows, LANES)
    parts = pl.pallas_call(
        functools.partial(kernel, rows * lax.axis_size("lat")),
        out_shape=(out(*cube),) * 4 + (out(FLAT, nt + 1, count + SUB, LANES),),
        in_specs=[far] * 9,
        out_specs=(block,) * 5,
        scratch_shapes=(
            [own, own, raw, raw] + [wide] * 5 + [own, own, raw, raw, own]
            + [vmem(nt, rows, LANES)] * 2 + [ints] * 2
            + [vmem(nt + 1, erows + SUB, LANES)] + [vmem(nt + 1, erows, LANES)] * 2
            + [vmem(FLAT, nt, erows, LANES)]
            + [vmem(rows // SUB, SUB, LANES)] * 2
            + [vmem(2, rows, LANES), vmem(2, erows, LANES), vmem(2, erows, LANES)]
            + [vmem(rows, LANES), vmem(erows, LANES), vmem(erows, LANES)]
            + [pltpu.SemaphoreType.DMA((9 * nt,))]
            + [pltpu.SemaphoreType.DMA((n1,))] * 2
            + [pltpu.SemaphoreType.DMA((n2,))] * 2
        ),
        compiler_params=pltpu.CompilerParams(
            collective_id=0, has_side_effects=True, vmem_limit_bytes=32 * 1024 * 1024),
    )(*[pltpu.with_memory_space_constraint(a, pltpu.HBM) for a in args])
    cube, plane = (levels, rows, cols), (rows, cols)
    return pl.pallas_call(
        tail,
        out_shape=(pltpu.HBM(cube, F32),) * 4 + (pltpu.HBM(plane, F32),) * 3,
        in_specs=[block] * 5,
        out_specs=(far,) * 7,
        scratch_shapes=(
            [vmem(nt + 1, count + 2 * SUB, LANES)] * 3 + [vmem(nt + 1, count, LANES)] * 2
            + [own, own, vmem(4, nt, rows, LANES)]
            + [pltpu.SemaphoreType.DMA((7 * nt,))]
        ),
        compiler_params=pltpu.CompilerParams(vmem_limit_bytes=32 * 1024 * 1024),
    )(*parts)


def solution(mesh):
    cube, plane = P(None, "lat", "lon"), P("lat", "lon")
    return jax.shard_map(
        body,
        mesh=mesh,
        in_specs=(cube,) * 4 + (plane,) * 5,
        out_specs=(cube,) * 4 + (plane,) * 3,
        check_vma=False,
    )
```

profile of v0, /device:TPU:0, one launch (start us, length us, event | category | flops | bytes accessed | tf_op | source)
XLA Modules:
  0.0 23.9 jit_solution(5890030187414796469)
XLA Ops:
  0.6 21.2 %shard_map.144 = (f32[12,3,32,128]{3,2,1,0:T(8,128)S(1)}, f32[12,3,32,128]{3,2,1,0:T(8,128)S(1)}, f32[12,3,32,128]{3,2,1,0:T(8,128)S(1)}, f32[12,3,32,128]{3,2,1,0:T(8,128)S(1)}, f32[6,4,48,128]{3,2,1,0:T(8,128)S(1)}) custom-call(f32[12,32,384]{2,1,0:T(8,128)} %t_in.1, f32[12,32,384]{2,1,0:T(8,128)} %s_in.1, f32[12,32,384]{2,1,0:T(8,128)} %u_in.1, ...), custom_call_target="tpu_custom_call" | custom-call | tf_op jit(solution)/shard_map/pallas_call | solution.py:589
  21.9 2.1 %shard_map.145 = (f32[12,32,384]{2,1,0:T(8,128)}, f32[12,32,384]{2,1,0:T(8,128)}, f32[12,32,384]{2,1,0:T(8,128)}, f32[12,32,384]{2,1,0:T(8,128)}, f32[32,384]{1,...) custom-call(f32[12,3,32,128]{3,2,1,0:T(8,128)S(1)} %get-tuple-element.12.t, ...), custom_call_target="tpu_custom_call" | custom-call | tf_op jit(solution)/shard_map/pallas_call | solution.py:610
where the time goes:
time: 24.1 us; the launch traced here: 23.9 us
  Pallas kernels  23.3 us (97%)
  between operations  0.64 us (3%)
    pallas_call x1, Pallas kernels, body(): pl.pallas_call(functools.partial(kernel, rows * lax.axis_size('lat')), ou...  21.2 us
    pallas_call x1, Pallas kernels, body(): pl.pallas_call(tail, out_shape=(pltpu.HBM(cube, F32),) * 4 + (pltpu.HBM(p...  2.05 us

commit v1 on v0

--- a/solution.py
+++ b/solution.py
@@ -69,6 +69,16 @@
     return carry
 
 
+def east_in(x, lane, s):
+    r = pltpu.roll(x, LANES - s, 2)
+    return jnp.where(lane < LANES - s, r, jnp.concatenate([r[1:], jnp.zeros_like(r[:1])], axis=0))
+
+
+def west_in(x, lane):
+    r = pltpu.roll(x, 1, 2)
+    return jnp.where(lane >= 1, r, jnp.concatenate([jnp.zeros_like(r[:1]), r[:-1]], axis=0))
+
+
 def face_weights(speed, opening):
     p = speed * (TIME_STEP / 12.0)
     q = jnp.abs(p)
@@ -83,7 +93,7 @@
     t_out, s_out, u_out, v_out, flat_out,
     tr, sr, ur, vr, tm, sm, um, vm, pm, xt, xs, yt, ys, ratio,
     zt, mt, wi, bi, de, hue, hve, flat, fu_ref, fv_ref,
-    strip1, fe1, fw1, strip2, fe2, fw2,
+    strip0, fe0, fw0, strip1, fe1, fw1, strip2, fe2, fw2, mend,
     load_sem, send1, recv1, send2, recv2,
 ):
     levels, nt, rows, _ = t_out.shape
@@ -96,6 +106,26 @@
     has_n, has_s = lat < nlat - 1, lat > 0
     own = pl.ds(SUB, rows)
 
+    barrier = pltpu.get_barrier_semaphore()
+
+    def greet(lo, la):
+        pl.semaphore_signal(barrier, inc=1, device_id=(lo, la), device_id_type=MESH)
+
+    greet(wst, lat)
+    greet(est, lat)
+
+    @pl.when(has_n)
+    def _():
+        greet(wst, nth)
+        greet(lon, nth)
+        greet(est, nth)
+
+    @pl.when(has_s)
+    def _():
+        greet(wst, sth)
+        greet(lon, sth)
+        greet(est, sth)
+
     loads = []
 
     def load(src, dst):
@@ -110,8 +140,8 @@
 
     ld_wi = load(lambda s: wi_in.at[:, s], lambda c: wi.at[c])
     ld_bi = load(lambda s: bi_in.at[:, s], lambda c: bi.at[c])
-    ld_t = load(lambda s: t_in.at[:, :, s], lambda c: tr.at[:, c])
-    ld_s = load(lambda s: s_in.at[:, :, s], lambda c: sr.at[:, c])
+    ld_t = load(lambda s: t_in.at[:, :, s], lambda c: tr.at[:, c, own, :])
+    ld_s = load(lambda s: s_in.at[:, :, s], lambda c: sr.at[:, c, own, :])
     ld_u = load(lambda s: u_in.at[:, :, s], lambda c: ur.at[:, c, own, :])
     ld_v = load(lambda s: v_in.at[:, :, s], lambda c: vr.at[:, c, own, :])
     ld_e = load(lambda s: eta_in.at[:, s], lambda c: flat.at[0, c, own, :])
@@ -123,41 +153,23 @@
             for c in g:
                 c.wait()
 
-    de[:, 0:SUB, :] = jnp.zeros((nt + 1, SUB, LANES), F32)
-    de[:, end:, :] = jnp.zeros((nt + 1, 2 * SUB, LANES), F32)
-    for ref in (fe1, fw1):
-        ref[:, 0:SUB, :] = jnp.zeros((2, SUB, LANES), F32)
-        ref[:, end:, :] = jnp.zeros((2, SUB, LANES), F32)
-    for ref in (fe2, fw2):
-        ref[0:SUB, :] = jnp.zeros((SUB, LANES), F32)
-        ref[end:, :] = jnp.zeros((SUB, LANES), F32)
-    for f in range(FLAT):
-        flat[f, :, 0:SUB, :] = jnp.zeros((nt, SUB, LANES), F32)
-        flat[f, :, end:, :] = jnp.zeros((nt, SUB, LANES), F32)
-    for ref in (tm, sm):
-        for k in range(levels):
-            ref[k, 0:nt, 0:SUB, :] = jnp.zeros((nt, SUB, LANES), F32)
-            ref[k, 0:nt, end:, :] = jnp.zeros((nt, SUB, LANES), F32)
-
-    barrier = pltpu.get_barrier_semaphore()
-
-    def greet(lo, la):
-        pl.semaphore_signal(barrier, inc=1, device_id=(lo, la), device_id_type=MESH)
-
-    greet(wst, lat)
-    greet(est, lat)
-
-    @pl.when(has_n)
+    def clear(first):
+        beyond = slice(first, first + SUB)
+        de[:, beyond, :] = jnp.zeros((nt + 1, SUB, LANES), F32)
+        for ref in (fe0, fw0, fe2, fw2):
+            ref[beyond, :] = jnp.zeros((SUB, LANES), F32)
+        for ref in (fe1, fw1):
+            ref[:, beyond, :] = jnp.zeros((2, SUB, LANES), F32)
+        for f in range(FLAT):
+            flat[f, :, beyond, :] = jnp.zeros((nt, SUB, LANES), F32)
+
+    @pl.when(jnp.logical_not(has_s))
     def _():
-        greet(wst, nth)
-        greet(lon, nth)
-        greet(est, nth)
-
-    @pl.when(has_s)
+        clear(0)
+
+    @pl.when(jnp.logical_not(has_n))
     def _():
-        greet(wst, sth)
-        greet(lon, sth)
-        greet(est, sth)
+        clear(end)
 
     def copier(send, recv):
         made = []
@@ -219,10 +231,8 @@
         return ref.at[0:nt, pl.ds(first, n), :]
 
     depth_up, depth_down = [rows_up(de, 2, plane_rows)], [rows_down(de, 2, plane_rows)]
-    flow_up = [rows_up(r, 1, cube_rows) for r in (ur, vr)]
-    flow_down = [rows_down(r, 1, cube_rows) for r in (ur, vr)]
-    tracer_up = [rows_up(r, 2, cube_rows) for r in (tm, sm)]
-    tracer_down = [rows_down(r, 2, cube_rows) for r in (tm, sm)]
+    field_up = [rows_up(r, n, cube_rows) for r, n in ((tr, 2), (sr, 2), (ur, 1), (vr, 1))]
+    field_down = [rows_down(r, n, cube_rows) for r, n in ((tr, 2), (sr, 2), (ur, 1), (vr, 1))]
 
     def strips(cp, strip, fe, fw, at, n):
         along = [cp(at(strip, 0, rows), at(fe, SUB, rows), wst, lat),
@@ -233,6 +243,8 @@
                 cp(at(strip, 0, n), at(fw, end, n), est, sth)]
         return along, up, down
 
+    along0, corner_up0, corner_down0 = strips(
+        cp, strip0, fe0, fw0, lambda r, a, n: r.at[pl.ds(a, n), :], 2)
     along1, corner_up1, corner_down1 = strips(
         cp, strip1, fe1, fw1, lambda r, a, n: r.at[:, pl.ds(a, n), :], 2)
 
@@ -248,105 +260,114 @@
         at = LANES // 2 - (LANES // 2) % nr + nr + r
         fv_ref[r] = jnp.broadcast_to(f[:, at:at + 1], (SUB, LANES))
 
+    def edge(first, last, p):
+        return pltpu.roll(jnp.where(tall < LANES // 2, first, last), 4 * p + 2, 1)
+
     arrived(ld_wi, ld_bi)
     depth = (wi[...] * bi[...]).astype(F32)
     de[0:nt, own, :] = depth
-    arrived(ld_t, ld_s, ld_u, ld_v)
+    strip0[...] = edge(depth[0], depth[nt - 1], 0)
     pl.semaphore_wait(barrier, 2 + 3 * has_n.astype(jnp.int32) + 3 * has_s.astype(jnp.int32))
-    start_ns(depth_up, depth_down)
-    start_ns(flow_up, flow_down)
+    for c in along0:
+        c.start()
+    start_ns(depth_up + corner_up0, depth_down + corner_down0)
+    for n, group in enumerate((ld_t, ld_s, ld_u, ld_v)):
+        arrived(group)
+        start_ns(field_up[n:n + 1], field_down[n:n + 1])
+
+    HALF = 0.5 * GRAVITY_FACTOR * TIME_STEP
+
+    def pressure(t, s, total):
+        h = (HALF * HALINE_COEF) * s - (HALF * THERMAL_COEF) * t
+        p = total + h
+        return p, p + h
 
     place = lax.shift_right_logical(tall, 2)
-
-    def edge(first, last, p):
-        return pltpu.roll(jnp.where(tall < LANES // 2, first, last), 4 * p + 2, 1)
-
-    group_a = edge(depth[0], depth[nt - 1], 2 * levels)
+    group_a = jnp.zeros((rows, LANES), F32)
     group_b = jnp.zeros((rows, LANES), F32)
+    total = jnp.zeros((nt, rows, LANES), F32)
     for k in range(levels):
         wet = de[0:nt, own, :] > k
-        t = jnp.where(wet, tr[k], 0.0)
-        s = jnp.where(wet, sr[k], 0.0)
-        tm[k, 0:nt, own, :] = t
-        sm[k, 0:nt, own, :] = s
+        t = jnp.where(wet, tr[k, :, own, :], 0.0)
+        s = jnp.where(wet, sr[k, :, own, :], 0.0)
+        tm[k, :, own, :] = t
+        sm[k, :, own, :] = s
+        p, total = pressure(t, s, total)
+        pm[k, 0:nt, own, :] = p
         group_a = jnp.where(place == 2 * k, edge(t[0], t[nt - 1], 2 * k), group_a)
         group_a = jnp.where(place == 2 * k + 1, edge(s[0], s[nt - 1], 2 * k + 1), group_a)
         group_b = jnp.where(place == 2 * k, edge(ur[k, 0, own, :], ur[k, nt - 1, own, :], 2 * k), group_b)
         group_b = jnp.where(place == 2 * k + 1, edge(vr[k, 0, own, :], vr[k, nt - 1, own, :], 2 * k + 1), group_b)
+        group_b = jnp.where(tall == 8 * k + 7, pltpu.roll(p[0], 8 * k + 7, 1), group_b)
     strip1[0] = group_a
     strip1[1] = group_b
     for c in along1:
         c.start()
     start_ns(corner_up1, corner_down1)
-    start_ns(tracer_up, tracer_down)
-
-    HALF = 0.5 * GRAVITY_FACTOR * TIME_STEP
-
-    def pressure(t, s, total):
-        h = (HALF * HALINE_COEF) * s - (HALF * THERMAL_COEF) * t
-        p = total + h
-        return p, p + h
-
-    def own_pressure(k, total):
-        p, total = pressure(tm[k, 0:nt, own, :], sm[k, 0:nt, own, :], total)
-        pm[k, 0:nt, own, :] = p
-        return total
-
-    lax.fori_loop(0, levels, own_pressure, jnp.zeros((nt, rows, LANES), F32))
     arrived(ld_e, ld_z, ld_m)
     flat[5, :, own, :] = depth
 
-    for c in along1:
+    for c in along0:
         c.wait_recv()
-    recv_ns(corner_up1, corner_down1)
-    recv_ns(depth_up, depth_down)
-
-    pair = (lane_of((end + SUB, LANES)) & 3) >= 2
-    halo_a = jnp.where(pair, fe1[0], fw1[0])
-    halo_b = jnp.where(pair, fe1[1], fw1[1])
-    fe1[0] = halo_a
-    fe1[1] = halo_b
-    de[nt, 0:end + SUB, :] = pltpu.roll(halo_a, LANES - (8 * levels + 2), 1)
+    recv_ns(depth_up + corner_up0, depth_down + corner_down0)
+    high = lane_of((end + SUB, LANES))
+    pair = (high & 3) >= 2
+    de[nt, 0:end + SUB, :] = pltpu.roll(jnp.where(pair, fe0[...], fw0[...]), LANES - 2, 1)
     for r in range(0, end + SUB, SUB):
         d = de[:, r:r + SUB, :]
         hue[:, r:r + SUB, :] = jnp.minimum(d, east_all(d, lane))
         hve[:, r:r + SUB, :] = jnp.minimum(d, de[:, r + 1:r + SUB + 1, :])
-
-    def edges(k, total):
-        kf = k.astype(F32)
-        back = LANES - 2 - 8 * k
-        a = fe1[0, own, :]
-        t = pltpu.roll(a, back, 1)
-        s = pltpu.roll(a, back - 4, 1)
-        tm[k, nt, own, :] = t
-        sm[k, nt, own, :] = s
-        p, total = pressure(t, s, total)
-        pm[k, nt, own, :] = p
-        b = fe1[1]
-        um[k, nt] = jnp.where(hue[nt] > kf, pltpu.roll(b, back, 1), 0.0)
-        vm[k, nt] = jnp.where(hve[nt] > kf, pltpu.roll(b, back - 4, 1), 0.0)
-        um[k, 0:nt, own, :] = jnp.where(hue[0:nt, own, :] > kf, ur[k, :, own, :], 0.0)
-        vm[k, 0:nt, own, :] = jnp.where(hve[0:nt, own, :] > kf, vr[k, :, own, :], 0.0)
-        return total
-
-    total = jnp.zeros((rows, LANES), F32)
-    for k in range(levels):
-        total = edges(jnp.int32(k), total)
 
     @pl.loop(0, levels)
     def _(k):
         kf = k.astype(F32)
         for r in range(SUB, end, SUB):
             here = slice(r, r + SUB)
-            w0, w1, w2, w3 = face_weights(um[k, :, here, :], hue[:, here, :] > kf)
+            opening = hue[0:nt, here, :] > kf
+            u = jnp.where(opening, ur[k, :, here, :], 0.0)
+            um[k, 0:nt, here, :] = u
+            vm[k, 0:nt, here, :] = jnp.where(hve[0:nt, here, :] > kf, vr[k, :, here, :], 0.0)
+            w0, w1, w2, w3 = face_weights(u, opening)
             for ref, to in ((tm, xt), (sm, xs)):
                 c = ref[k, :, here, :]
-                fx = (w0 * c + w1 * east_all(c, lane)
-                      - w2 * east_all(c, lane, 2) + w3 * west_all(c, lane))
-                to[k, :, r - SUB:r, :] = c[:nt] - (fx[:nt] - west(fx, lane))
-
-    recv_ns(flow_up, flow_down)
-    recv_ns(tracer_up, tracer_down)
+                fx = (w0 * c + w1 * east_in(c, lane, 1)
+                      - w2 * east_in(c, lane, 2) + w3 * west_in(c, lane))
+                to[k, :, r - SUB:r, :] = c - (fx - west_in(fx, lane))
+
+    for c in along1:
+        c.wait_recv()
+    recv_ns(corner_up1, corner_down1)
+    halo_b = jnp.where(pair, fe1[1], fw1[1])
+    for k in range(levels):
+        back = LANES - 2 - 8 * k
+        um[k, nt] = jnp.where(hue[nt] > k, pltpu.roll(halo_b, back, 1), 0.0)
+        vm[k, nt] = jnp.where(hve[nt] > k, pltpu.roll(halo_b, back - 4, 1), 0.0)
+        pm[k, nt, own, :] = pltpu.roll(halo_b[SUB:end], back - 5, 1)
+
+    q = tall & 3
+    level = lax.shift_right_logical(tall, 3).astype(F32)
+
+    def column(c, at):
+        return jnp.broadcast_to(hue[c, own, at:at + 1], (rows, LANES))
+
+    def speeds(x, limit):
+        x = jnp.where((tall & 7) < 4, x, pltpu.roll(x, 4, 1))
+        opening = limit > level
+        return face_weights(jnp.where(opening, x, 0.0), opening)
+
+    mine = strip1[0]
+    a = jnp.where(q < 2, mine, fe1[0, own, :])
+    b = jnp.where(q < 2, fw1[0, own, :], mine)
+    _, w1, w2, w3 = speeds(strip1[1], jnp.where(
+        q == 0, column(nt - 1, LANES - 2), jnp.where(q == 1, column(nt - 1, LANES - 1), column(0, 0))))
+    b_west = pltpu.roll(b, 1, 1)
+    flux = jnp.where(q == 1, w1 * pltpu.roll(a, LANES - 1, 1), 0.0) - w2 * pltpu.roll(a, LANES - 2, 1)
+    flux = jnp.where(q < 2, flux, jnp.where(q == 2, w3 * b_west, 0.0))
+    w0, w1, w2, w3 = speeds(fw1[1, own, :], column(nt, LANES - 1))
+    first = w0 * b + w1 * pltpu.roll(b, LANES - 1, 1) - w2 * pltpu.roll(b, LANES - 2, 1) + w3 * b_west
+    mend[...] = flux - pltpu.roll(jnp.where(q == 1, first, flux), 1, 1)
+
+    recv_ns(field_up, field_down)
 
     def far_rows(k, total):
         kf = k.astype(F32)
@@ -354,8 +375,11 @@
             out = slice(a, a + SUB)
             um[k, 0:nt, out, :] = jnp.where(hue[0:nt, out, :] > kf, ur[k, :, out, :], 0.0)
             vm[k, 0:nt, out, :] = jnp.where(hve[0:nt, out, :] > kf, vr[k, :, out, :], 0.0)
+            wet = de[0:nt, out, :] > kf
+            tm[k, :, out, :] = jnp.where(wet, tr[k, :, out, :], 0.0)
+            sm[k, :, out, :] = jnp.where(wet, sr[k, :, out, :], 0.0)
         out = slice(end, end + SUB)
-        p, total = pressure(tm[k, 0:nt, out, :], sm[k, 0:nt, out, :], total)
+        p, total = pressure(tm[k, :, out, :], sm[k, :, out, :], total)
         pm[k, 0:nt, out, :] = p
         return total
 
@@ -427,8 +451,14 @@
             w0, w1, w2, w3 = face_weights(vm[k, 0:nt, here, :], hve[0:nt, here, :] > kf)
             for ref, to in ((tm, yt), (sm, ys)):
                 to[k, :, here, :] = (
-                    w0 * ref[k, 0:nt, here, :] + w1 * ref[k, 0:nt, a + 1:a + SUB + 1, :]
-                    - w2 * ref[k, 0:nt, a + 2:a + SUB + 2, :] + w3 * ref[k, 0:nt, a - 1:a + SUB - 1, :])
+                    w0 * ref[k, :, here, :] + w1 * ref[k, :, a + 1:a + SUB + 1, :]
+                    - w2 * ref[k, :, a + 2:a + SUB + 2, :] + w3 * ref[k, :, a - 1:a + SUB - 1, :])
+
+    def mended(x, m):
+        edge_lane = lane_of(m.shape)
+        first = x[:1] - jnp.where(edge_lane < 2, m, 0.0)[None]
+        last = x[-1:] - jnp.where(edge_lane >= LANES - 2, m, 0.0)[None]
+        return jnp.concatenate([first, x[1:-1], last], axis=0)
 
     span = 2 * SUB if rows % (2 * SUB) == 0 else SUB
     DIFF = TIME_STEP * STABILITY_FACTOR * BACKGROUND_MIX
@@ -440,6 +470,8 @@
         def star(k):
             t = xt[k, :, out, :] - (yt[k, :, here, :] - yt[k, :, below, :])
             s = xs[k, :, out, :] - (ys[k, :, here, :] - ys[k, :, below, :])
+            t = mended(t, pltpu.roll(mend[out, :], LANES - 2 - 8 * k, 1))
+            s = mended(s, pltpu.roll(mend[out, :], LANES - 6 - 8 * k, 1))
             return t, s, HALINE_COEF * s - THERMAL_COEF * t
 
         def forward(k, carry):
@@ -489,10 +521,10 @@
         flat_out[f, nt, 0:count] = pltpu.roll(halo, LANES - 8 * f - 4, 1)
     flat_out[5, :, count:, :] = jnp.zeros((nt + 1, SUB, LANES), F32)
 
-    for c in along1 + along2:
+    for c in along0 + along1 + along2:
         c.wait_send()
-    sent_ns(depth_up + flow_up + tracer_up + corner_up1 + flat_up + corner_up2,
-            depth_down + flow_down + tracer_down + corner_down1 + flat_down + corner_down2)
+    sent_ns(depth_up + corner_up0 + field_up + corner_up1 + flat_up + corner_up2,
+            depth_down + corner_down0 + field_down + corner_down1 + flat_down + corner_down2)
 
 
 def tail(
@@ -584,7 +616,7 @@
     own = vmem(levels, nt, rows, LANES)
     wide = vmem(levels, nt + 1, erows, LANES)
     ints = pltpu.VMEM((nt, rows, LANES), jnp.int32)
-    n1, n2 = 2 + 4 + 4 + 6, 2 + 6
+    n1, n2 = 2 + 8 + 6 + 6, 2 + 6
     cube = (levels, nt, rows, LANES)
     parts = pl.pallas_call(
         functools.partial(kernel, rows * lax.axis_size("lat")),
@@ -592,13 +624,14 @@
         in_specs=[far] * 9,
         out_specs=(block,) * 5,
         scratch_shapes=(
-            [own, own, raw, raw] + [wide] * 5 + [own, own, raw, raw, own]
+            [raw] * 6 + [wide] * 3 + [own, own, raw, raw, own]
             + [vmem(nt, rows, LANES)] * 2 + [ints] * 2
             + [vmem(nt + 1, erows + SUB, LANES)] + [vmem(nt + 1, erows, LANES)] * 2
             + [vmem(FLAT, nt, erows, LANES)]
             + [vmem(rows // SUB, SUB, LANES)] * 2
+            + [vmem(rows, LANES), vmem(erows, LANES), vmem(erows, LANES)]
             + [vmem(2, rows, LANES), vmem(2, erows, LANES), vmem(2, erows, LANES)]
-            + [vmem(rows, LANES), vmem(erows, LANES), vmem(erows, LANES)]
+            + [vmem(rows, LANES), vmem(erows, LANES), vmem(erows, LANES), vmem(rows, LANES)]
             + [pltpu.SemaphoreType.DMA((9 * nt,))]
             + [pltpu.SemaphoreType.DMA((n1,))] * 2
             + [pltpu.SemaphoreType.DMA((n2,))] * 2

time: 24.1 us -> 23.1 us (0.959)
  Pallas kernels: 23.3 us -> 22.3 us
    pallas_call x1, Pallas kernels: 21.2 us -> 20.3 us  [body(): pl.pallas_call(functools.partial(kernel, rows * lax.axis_size('lat')), ou...]
where the time goes in v1:
time: 23.1 us; the launch traced here: 23 us
  Pallas kernels  22.3 us (97%)
  between operations  0.64 us (3%)
    pallas_call x1, Pallas kernels, body(): pl.pallas_call(functools.partial(kernel, rows * lax.axis_size('lat')), ou...  20.3 us
    pallas_call x1, Pallas kernels, body(): pl.pallas_call(tail, out_shape=(pltpu.HBM(cube, F32),) * 4 + (pltpu.HBM(p...  2.05 us

profile of v1, /device:TPU:0, one launch (start us, length us, event | category | flops | bytes accessed | tf_op | source)
XLA Modules:
  0.0 23.0 jit_solution(11803533808866065828)
XLA Ops:
  0.6 20.3 %shard_map.144 = (f32[12,3,32,128]{3,2,1,0:T(8,128)S(1)}, f32[12,3,32,128]{3,2,1,0:T(8,128)S(1)}, f32[12,3,32,128]{3,2,1,0:T(8,128)S(1)}, f32[12,3,32,128]{3,2,1,0:T(8,128)S(1)}, f32[6,4,48,128]{3,2,1,0:T(8,128)S(1)}) custom-call(f32[12,32,384]{2,1,0:T(8,128)} %t_in.1, f32[12,32,384]{2,1,0:T(8,128)} %s_in.1, f32[12,32,384]{2,1,0:T(8,128)} %u_in.1, ...), custom_call_target="tpu_custom_call" | custom-call | tf_op jit(solution)/shard_map/pallas_call | solution.py:621
  20.9 2.1 %shard_map.145 = (f32[12,32,384]{2,1,0:T(8,128)}, f32[12,32,384]{2,1,0:T(8,128)}, f32[12,32,384]{2,1,0:T(8,128)}, f32[12,32,384]{2,1,0:T(8,128)}, f32[32,384]{1,...) custom-call(f32[12,3,32,128]{3,2,1,0:T(8,128)S(1)} %get-tuple-element.12.t, ...), custom_call_target="tpu_custom_call" | custom-call | tf_op jit(solution)/shard_map/pallas_call | solution.py:643

commit v2 on v1

--- a/solution.py
+++ b/solution.py
@@ -91,13 +91,14 @@
     lat_total,
     t_in, s_in, u_in, v_in, eta_in, zt_in, mt_in, wi_in, bi_in,
     t_out, s_out, u_out, v_out, flat_out,
-    tr, sr, ur, vr, tm, sm, um, vm, pm, xt, xs, yt, ys, ratio,
+    tr, sr, ur, vr, tm, sm, um, vm, pm, wu, ev, xt, xs, yt, ys, ratio,
     zt, mt, wi, bi, de, hue, hve, flat, fu_ref, fv_ref,
-    strip0, fe0, fw0, strip1, fe1, fw1, strip2, fe2, fw2, mend,
+    strip0, fe0, fw0, strip1, fe1, fw1, strip2, fe2, fw2, mend, edge_b, acc,
     load_sem, send1, recv1, send2, recv2,
 ):
     levels, nt, rows, _ = t_out.shape
     end = SUB + rows
+    zero = jnp.zeros((nt, SUB, LANES), F32)
     nr = rows // SUB
     lon, lat = lax.axis_index("lon"), lax.axis_index("lat")
     nlon, nlat = lax.axis_size("lon"), lax.axis_size("lat")
@@ -251,6 +252,15 @@
     lane = lane_of((SUB, LANES))
     tall = lane_of((rows, LANES))
 
+    for k in range(levels):
+        for ref in (um, vm):
+            ref[k, :, 0:SUB, :] = zero
+            ref[k, :, end:, :] = zero
+        pm[k, :, end:, :] = zero
+        wu[k, :, end:, :] = zero
+        ev[k, :, 0:SUB, :] = zero
+    acc[...] = jnp.zeros_like(acc)
+
     sub = lax.broadcasted_iota(jnp.int32, (SUB, LANES), 0)
     j = (lat * rows + sub + SUB * lax.rem(lane, nr)).astype(F32)
     j = j + jnp.where(lane < LANES // 2, 0.5, 1.0)
@@ -259,6 +269,8 @@
         fu_ref[r] = jnp.broadcast_to(f[:, r:r + 1], (SUB, LANES))
         at = LANES // 2 - (LANES // 2) % nr + nr + r
         fv_ref[r] = jnp.broadcast_to(f[:, at:at + 1], (SUB, LANES))
+    fu_south = jnp.broadcast_to(f[0:1, 0:1], (SUB, LANES))
+    fv_north = jnp.broadcast_to(f[SUB - 1:SUB, at:at + 1], (SUB, LANES))
 
     def edge(first, last, p):
         return pltpu.roll(jnp.where(tall < LANES // 2, first, last), 4 * p + 2, 1)
@@ -293,7 +305,7 @@
         tm[k, :, own, :] = t
         sm[k, :, own, :] = s
         p, total = pressure(t, s, total)
-        pm[k, 0:nt, own, :] = p
+        pm[k, :, own, :] = p
         group_a = jnp.where(place == 2 * k, edge(t[0], t[nt - 1], 2 * k), group_a)
         group_a = jnp.where(place == 2 * k + 1, edge(s[0], s[nt - 1], 2 * k + 1), group_a)
         group_b = jnp.where(place == 2 * k, edge(ur[k, 0, own, :], ur[k, nt - 1, own, :], 2 * k), group_b)
@@ -318,112 +330,135 @@
         hue[:, r:r + SUB, :] = jnp.minimum(d, east_all(d, lane))
         hve[:, r:r + SUB, :] = jnp.minimum(d, de[:, r + 1:r + SUB + 1, :])
 
+    MIX = TIME_STEP * MOMENTUM_DIFF
+    KEEP = 1.0 - TIME_STEP * BOTTOM_DRAG - 4.0 * MIX
+
     @pl.loop(0, levels)
     def _(k):
         kf = k.astype(F32)
-        for r in range(SUB, end, SUB):
-            here = slice(r, r + SUB)
-            opening = hue[0:nt, here, :] > kf
-            u = jnp.where(opening, ur[k, :, here, :], 0.0)
-            um[k, 0:nt, here, :] = u
-            vm[k, 0:nt, here, :] = jnp.where(hve[0:nt, here, :] > kf, vr[k, :, here, :], 0.0)
-            w0, w1, w2, w3 = face_weights(u, opening)
-            for ref, to in ((tm, xt), (sm, xs)):
-                c = ref[k, :, here, :]
-                fx = (w0 * c + w1 * east_in(c, lane, 1)
-                      - w2 * east_in(c, lane, 2) + w3 * west_in(c, lane))
-                to[k, :, r - SUB:r, :] = c - (fx - west_in(fx, lane))
-
-    for c in along1:
-        c.wait_recv()
-    recv_ns(corner_up1, corner_down1)
-    halo_b = jnp.where(pair, fe1[1], fw1[1])
-    for k in range(levels):
-        back = LANES - 2 - 8 * k
-        um[k, nt] = jnp.where(hue[nt] > k, pltpu.roll(halo_b, back, 1), 0.0)
-        vm[k, nt] = jnp.where(hve[nt] > k, pltpu.roll(halo_b, back - 4, 1), 0.0)
-        pm[k, nt, own, :] = pltpu.roll(halo_b[SUB:end], back - 5, 1)
-
-    q = tall & 3
-    level = lax.shift_right_logical(tall, 3).astype(F32)
-
-    def column(c, at):
-        return jnp.broadcast_to(hue[c, own, at:at + 1], (rows, LANES))
-
-    def speeds(x, limit):
-        x = jnp.where((tall & 7) < 4, x, pltpu.roll(x, 4, 1))
-        opening = limit > level
-        return face_weights(jnp.where(opening, x, 0.0), opening)
-
-    mine = strip1[0]
-    a = jnp.where(q < 2, mine, fe1[0, own, :])
-    b = jnp.where(q < 2, fw1[0, own, :], mine)
-    _, w1, w2, w3 = speeds(strip1[1], jnp.where(
-        q == 0, column(nt - 1, LANES - 2), jnp.where(q == 1, column(nt - 1, LANES - 1), column(0, 0))))
-    b_west = pltpu.roll(b, 1, 1)
-    flux = jnp.where(q == 1, w1 * pltpu.roll(a, LANES - 1, 1), 0.0) - w2 * pltpu.roll(a, LANES - 2, 1)
-    flux = jnp.where(q < 2, flux, jnp.where(q == 2, w3 * b_west, 0.0))
-    w0, w1, w2, w3 = speeds(fw1[1, own, :], column(nt, LANES - 1))
-    first = w0 * b + w1 * pltpu.roll(b, LANES - 1, 1) - w2 * pltpu.roll(b, LANES - 2, 1) + w3 * b_west
-    mend[...] = flux - pltpu.roll(jnp.where(q == 1, first, flux), 1, 1)
-
-    recv_ns(field_up, field_down)
-
-    def far_rows(k, total):
+        um[k, :, own, :] = jnp.where(hue[0:nt, own, :] > kf, ur[k, :, own, :], 0.0)
+        vm[k, :, own, :] = jnp.where(hve[0:nt, own, :] > kf, vr[k, :, own, :], 0.0)
+
+    @pl.loop(0, levels)
+    def _(k):
         kf = k.astype(F32)
-        for a in (0, end):
-            out = slice(a, a + SUB)
-            um[k, 0:nt, out, :] = jnp.where(hue[0:nt, out, :] > kf, ur[k, :, out, :], 0.0)
-            vm[k, 0:nt, out, :] = jnp.where(hve[0:nt, out, :] > kf, vr[k, :, out, :], 0.0)
-            wet = de[0:nt, out, :] > kf
-            tm[k, :, out, :] = jnp.where(wet, tr[k, :, out, :], 0.0)
-            sm[k, :, out, :] = jnp.where(wet, sr[k, :, out, :], 0.0)
-        out = slice(end, end + SUB)
-        p, total = pressure(tm[k, :, out, :], sm[k, :, out, :], total)
-        pm[k, 0:nt, out, :] = p
-        return total
-
-    step_loop(0, levels, 2, far_rows, jnp.zeros((nt, SUB, LANES), F32))
-
-    MIX = TIME_STEP * MOMENTUM_DIFF
-    KEEP = 1.0 - TIME_STEP * BOTTOM_DRAG - 4.0 * MIX
-    for r in range(nr):
-        at = SUB + SUB * r
-        here, above, below = slice(at, at + SUB), slice(at + 1, at + SUB + 1), slice(at - 1, at + SUB - 1)
-        out = slice(SUB * r, SUB * r + SUB)
-
-        def momentum(k, carry, wind=None):
-            su, sv, tu, tv = carry
-            kf = k.astype(F32)
-            u4, un = um[k, :, here, :], um[k, :, above, :]
-            v4, vs = vm[k, :, here, :], vm[k, :, below, :]
-            u, v = u4[:nt], v4[:nt]
-            around_u = east(u4, lane) + west(u4, lane) + un[:nt] + um[k, 0:nt, below, :]
-            around_v = east(v4, lane) + west(v4, lane) + vs[:nt] + vm[k, 0:nt, above, :]
-            a, b = v4 + vs, u4 + un
-            vbar = a[:nt] + east(a, lane)
-            ubar = b[:nt] + west(b, lane)
+        for at in range(SUB, end, SUB):
+            here = slice(at, at + SUB)
+            wu[k, :, here, :] = west_in(um[k, :, here, :], lane)
+            ev[k, :, here, :] = east_in(vm[k, :, here, :], lane, 1)
+        for r in range(nr):
+            at = SUB + SUB * r
+            here, above, below = slice(at, at + SUB), slice(at + 1, at + SUB + 1), slice(at - 1, at + SUB - 1)
+            out = slice(SUB * r, SUB * r + SUB)
+            u, un, w = um[k, :, here, :], um[k, :, above, :], wu[k, :, here, :]
+            v, vs, e = vm[k, :, here, :], vm[k, :, below, :], ev[k, :, here, :]
             p = pm[k, :, here, :]
-            px = east(p, lane) - p[:nt]
-            py = pm[k, 0:nt, above, :] - p[:nt]
-            ut = KEEP * u + MIX * around_u + fu_ref[r] * vbar - px
-            vt = KEEP * v + MIX * around_v - fv_ref[r] * ubar - py
-            if wind is not None:
-                ut = ut + wind * zt[:, out, :]
-                vt = vt + wind * mt[:, out, :]
+            around_u = (east_in(u, lane, 1) + w) + (un + um[k, :, below, :])
+            around_v = (west_in(v, lane) + e) + (vs + vm[k, :, above, :])
+            vbar = (v + vs) + (e + ev[k, :, below, :])
+            ubar = (u + un) + (w + wu[k, :, above, :])
+            ut = KEEP * u + MIX * around_u + fu_ref[r] * vbar - (east_in(p, lane, 1) - p)
+            vt = KEEP * v + MIX * around_v - fv_ref[r] * ubar - (pm[k, :, above, :] - p)
             ut = jnp.where(hue[0:nt, here, :] > kf, ut, 0.0)
             vt = jnp.where(hve[0:nt, here, :] > kf, vt, 0.0)
             u_out[k, :, out, :] = ut
             v_out[k, :, out, :] = vt
-            return su + u, sv + v, tu + ut, tv + vt
-
-        zero = jnp.zeros((nt, SUB, LANES), F32)
-        carry = momentum(jnp.int32(0), (zero,) * 4, TIME_STEP * WIND_FACTOR)
-        su, sv, tu, tv = step_loop(1, levels, 2, momentum, carry)
-        flat[1, :, here, :] = su
-        flat[2, :, here, :] = sv
-        flat[3, :, here, :] = tu - su
-        flat[4, :, here, :] = tv - sv
+            for n, x in enumerate((u, v, ut, vt)):
+                acc[n, :, out, :] += x
+
+    wind_u = jnp.where(hue[0:nt, own, :] > 0.0, (TIME_STEP * WIND_FACTOR) * zt[...], 0.0)
+    wind_v = jnp.where(hve[0:nt, own, :] > 0.0, (TIME_STEP * WIND_FACTOR) * mt[...], 0.0)
+    u_out[0, :, 0:rows, :] += wind_u
+    v_out[0, :, 0:rows, :] += wind_v
+    flat[1, :, own, :] = acc[0]
+    flat[2, :, own, :] = acc[1]
+    flat[3, :, own, :] = acc[2] - acc[0] + wind_u
+    flat[4, :, own, :] = acc[3] - acc[1] + wind_v
+
+    for c in along1:
+        c.wait_recv()
+    recv_ns(corner_up1, corner_down1)
+    level = lax.shift_right_logical(tall, 3).astype(F32)
+
+    def by_lane(at, one, two, five, six):
+        return jnp.where(at == 1, one, jnp.where(at == 2, two, jnp.where(at == 5, five, six)))
+
+    def column(ref, c, at, which=own, n=rows):
+        return jnp.broadcast_to(ref[c, which, at:at + 1], (n, LANES))
+
+    LAST = LANES - 1
+    for r in range(0, end + SUB, SUB):
+        here = slice(r, r + SUB)
+        limit = by_lane(lane & 7, *(column(ref, nt, at, here, SUB) for ref in (hue, hve) for at in (LAST, 0)))
+        limit = jnp.where((lane & 7) == 7, float(levels), limit)
+        x = jnp.where((lane & 3) >= 2, fe1[1, here, :], fw1[1, here, :])
+        edge_b[here, :] = jnp.where(limit > lax.shift_right_logical(lane, 3).astype(F32), x, 0.0)
+    x = edge_b[own, :]
+    spot = tall & 7
+    near = jnp.where((spot & 1) == 1, pltpu.roll(x, LAST, 1), pltpu.roll(x, 1, 1))
+    above, below = slice(SUB + 1, end + 1), slice(SUB - 1, end - 1)
+    turn_u = fu_ref[...].reshape(rows, LANES) * pltpu.roll(x + edge_b[below, :], LANES - 5, 1) - pltpu.roll(x, LANES - 6, 1)
+    turn_v = fv_ref[...].reshape(rows, LANES) * pltpu.roll(x + edge_b[above, :], 5, 1)
+    extra = MIX * near + jnp.where(spot == 1, turn_u, 0.0) - jnp.where(spot == 6, turn_v, 0.0)
+    limit = by_lane(spot, column(hue, nt - 1, LAST), column(hue, 0, 0), column(hve, nt - 1, LAST), column(hve, 0, 0))
+    extra = jnp.where(limit > level, extra, 0.0)
+    total_u = jnp.zeros((rows, LANES), F32)
+    total_v = jnp.zeros((rows, LANES), F32)
+    for k in range(levels):
+        du = pltpu.roll(extra, LANES - 2 - 8 * k, 1)
+        dv = pltpu.roll(extra, LANES - 6 - 8 * k, 1)
+        for ref, d in ((u_out, du), (v_out, dv)):
+            ref[k, 0, 0:rows, :] += jnp.where(tall == 0, d, 0.0)
+            ref[k, nt - 1, 0:rows, :] += jnp.where(tall == LAST, d, 0.0)
+        total_u = total_u + du
+        total_v = total_v + dv
+    for f, d in ((3, total_u), (4, total_v)):
+        flat[f, 0, own, :] += jnp.where(tall == 0, d, 0.0)
+        flat[f, nt - 1, own, :] += jnp.where(tall == LAST, d, 0.0)
+
+    recv_ns(field_up, field_down)
+    top = lax.broadcasted_iota(jnp.int32, (SUB, LANES), 0) == 0
+
+    def far_rows(k, carry):
+        total, nu, nv, su, sv = carry
+        kf = k.astype(F32)
+        for a in (0, end):
+            out = slice(a, a + SUB)
+            wet = de[0:nt, out, :] > kf
+            tm[k, :, out, :] = jnp.where(wet, tr[k, :, out, :], 0.0)
+            sm[k, :, out, :] = jnp.where(wet, sr[k, :, out, :], 0.0)
+        out = slice(0, SUB)
+        vm[k, :, out, :] = jnp.where(hve[0:nt, out, :] > kf, vr[k, :, out, :], 0.0)
+
+        out = slice(end, end + SUB)
+        wet = de[0:nt, out, :] > kf
+        p, total = pressure(jnp.where(wet, tr[k, :, out, :], 0.0), jnp.where(wet, sr[k, :, out, :], 0.0), total)
+        u = jnp.where(hue[0:nt, out, :] > kf, ur[k, :, out, :], 0.0)
+        v = jnp.where(hve[0:nt, out, :] > kf, vr[k, :, out, :], 0.0)
+        edge_row = slice(end - 1, end + SUB - 1)
+        du = jnp.where(top & (hue[0:nt, edge_row, :] > kf), MIX * u, 0.0)
+        dv = jnp.where(top & (hve[0:nt, edge_row, :] > kf),
+                       MIX * v - fv_north * (u + west_in(u, lane)) - p, 0.0)
+        row = slice(rows - 1, rows + SUB - 1)
+        u_out[k, :, row, :] += du
+        v_out[k, :, row, :] += dv
+        nu, nv = nu + du, nv + dv
+
+        out = slice(SUB - 1, 2 * SUB - 1)
+        u = jnp.where(hue[0:nt, out, :] > kf, ur[k, :, out, :], 0.0)
+        v = jnp.where(hve[0:nt, out, :] > kf, vr[k, :, out, :], 0.0)
+        edge_row = slice(SUB, 2 * SUB)
+        du = jnp.where(top & (hue[0:nt, edge_row, :] > kf),
+                       MIX * u + fu_south * (v + east_in(v, lane, 1)), 0.0)
+        dv = jnp.where(top & (hve[0:nt, edge_row, :] > kf), MIX * v, 0.0)
+        u_out[k, :, 0:SUB, :] += du
+        v_out[k, :, 0:SUB, :] += dv
+        return total, nu, nv, su + du, sv + dv
+
+    _, nu, nv, su, sv = step_loop(0, levels, 2, far_rows, (zero,) * 5)
+    for f, north, south in ((3, nu, su), (4, nv, sv)):
+        flat[f, :, SUB:2 * SUB, :] += south
+        flat[f, :, end - SUB:end, :] += pltpu.roll(north, SUB - 1, 1)
 
     spot = lax.shift_right_logical(tall, 3)
     group = jnp.zeros((rows, LANES), F32)
@@ -446,13 +481,40 @@
     @pl.loop(0, levels)
     def _(k):
         kf = k.astype(F32)
+        for r in range(SUB, end, SUB):
+            here = slice(r, r + SUB)
+            w0, w1, w2, w3 = face_weights(um[k, :, here, :], hue[0:nt, here, :] > kf)
+            for ref, to in ((tm, xt), (sm, xs)):
+                c = ref[k, :, here, :]
+                fx = (w0 * c + w1 * east_in(c, lane, 1)
+                      - w2 * east_in(c, lane, 2) + w3 * west_in(c, lane))
+                to[k, :, r - SUB:r, :] = c - (fx - west_in(fx, lane))
         for a in starts:
             here = slice(a, a + SUB)
-            w0, w1, w2, w3 = face_weights(vm[k, 0:nt, here, :], hve[0:nt, here, :] > kf)
+            w0, w1, w2, w3 = face_weights(vm[k, :, here, :], hve[0:nt, here, :] > kf)
             for ref, to in ((tm, yt), (sm, ys)):
                 to[k, :, here, :] = (
                     w0 * ref[k, :, here, :] + w1 * ref[k, :, a + 1:a + SUB + 1, :]
                     - w2 * ref[k, :, a + 2:a + SUB + 2, :] + w3 * ref[k, :, a - 1:a + SUB - 1, :])
+
+    q = tall & 3
+
+    def speeds(x, limit):
+        x = jnp.where((tall & 7) < 4, x, pltpu.roll(x, 4, 1))
+        opening = limit > level
+        return face_weights(jnp.where(opening, x, 0.0), opening)
+
+    mine = strip1[0]
+    a = jnp.where(q < 2, mine, fe1[0, own, :])
+    b = jnp.where(q < 2, fw1[0, own, :], mine)
+    _, w1, w2, w3 = speeds(strip1[1], jnp.where(
+        q == 0, column(hue, nt - 1, LANES - 2), jnp.where(q == 1, column(hue, nt - 1, LAST), column(hue, 0, 0))))
+    b_west = pltpu.roll(b, 1, 1)
+    flux = jnp.where(q == 1, w1 * pltpu.roll(a, LANES - 1, 1), 0.0) - w2 * pltpu.roll(a, LANES - 2, 1)
+    flux = jnp.where(q < 2, flux, jnp.where(q == 2, w3 * b_west, 0.0))
+    w0, w1, w2, w3 = speeds(fw1[1, own, :], column(hue, nt, LAST))
+    first = w0 * b + w1 * pltpu.roll(b, LANES - 1, 1) - w2 * pltpu.roll(b, LANES - 2, 1) + w3 * b_west
+    mend[...] = flux - pltpu.roll(jnp.where(q == 1, first, flux), 1, 1)
 
     def mended(x, m):
         edge_lane = lane_of(m.shape)
@@ -589,8 +651,8 @@
     @pl.loop(0, levels)
     def _(k):
         kf = k.astype(F32)
-        un[k] = jnp.where(cor[2] > kf, ut[k] + cor[0], 0.0)
-        vn[k] = jnp.where(cor[3] > kf, vt[k] + cor[1], 0.0)
+        un[k] = jnp.where(cor[2] > kf, ut[k, :, 0:rows, :] + cor[0], 0.0)
+        vn[k] = jnp.where(cor[3] > kf, vt[k, :, 0:rows, :] + cor[1], 0.0)
 
     put(lambda c: un.at[:, c], lambda d: u_out.at[:, :, d])
     put(lambda c: vn.at[:, c], lambda d: v_out.at[:, :, d])
@@ -614,17 +676,16 @@
     far = pl.BlockSpec(memory_space=pltpu.HBM)
     raw = vmem(levels, nt, erows, LANES)
     own = vmem(levels, nt, rows, LANES)
-    wide = vmem(levels, nt + 1, erows, LANES)
     ints = pltpu.VMEM((nt, rows, LANES), jnp.int32)
     n1, n2 = 2 + 8 + 6 + 6, 2 + 6
     cube = (levels, nt, rows, LANES)
     parts = pl.pallas_call(
         functools.partial(kernel, rows * lax.axis_size("lat")),
-        out_shape=(out(*cube),) * 4 + (out(FLAT, nt + 1, count + SUB, LANES),),
+        out_shape=(out(*cube),) * 2 + (out(levels, nt, rows + SUB, LANES),) * 2 + (out(FLAT, nt + 1, count + SUB, LANES),),
         in_specs=[far] * 9,
         out_specs=(block,) * 5,
         scratch_shapes=(
-            [raw] * 6 + [wide] * 3 + [own, own, raw, raw, own]
+            [raw] * 11 + [own, own, raw, raw, own]
             + [vmem(nt, rows, LANES)] * 2 + [ints] * 2
             + [vmem(nt + 1, erows + SUB, LANES)] + [vmem(nt + 1, erows, LANES)] * 2
             + [vmem(FLAT, nt, erows, LANES)]
@@ -632,6 +693,7 @@
             + [vmem(rows, LANES), vmem(erows, LANES), vmem(erows, LANES)]
             + [vmem(2, rows, LANES), vmem(2, erows, LANES), vmem(2, erows, LANES)]
             + [vmem(rows, LANES), vmem(erows, LANES), vmem(erows, LANES), vmem(rows, LANES)]
+            + [vmem(erows, LANES), vmem(4, nt, rows, LANES)]
             + [pltpu.SemaphoreType.DMA((9 * nt,))]
             + [pltpu.SemaphoreType.DMA((n1,))] * 2
             + [pltpu.SemaphoreType.DMA((n2,))] * 2

time: 23.1 us -> 20.5 us (0.89)
  Pallas kernels: 22.3 us -> 19.7 us
    pallas_call x1, Pallas kernels: 20.3 us -> 17.6 us  [body(): pl.pallas_call(functools.partial(kernel, rows * lax.axis_size('lat')), ou...]
where the time goes in v2:
time: 20.5 us; the launch traced here: 20.3 us
  Pallas kernels  19.7 us (96%)
  between operations  0.64 us (3%)
    pallas_call x1, Pallas kernels, body(): pl.pallas_call(functools.partial(kernel, rows * lax.axis_size('lat')), ou...  17.6 us
    pallas_call x1, Pallas kernels, body(): pl.pallas_call(tail, out_shape=(pltpu.HBM(cube, F32),) * 4 + (pltpu.HBM(p...  2.1 us

profile of v2, /device:TPU:0, one launch (start us, length us, event | category | flops | bytes accessed | tf_op | source)
XLA Modules:
  0.0 20.3 jit_solution(18129885329213834323)
XLA Ops:
  0.6 17.6 %shard_map.144 = (f32[12,3,32,128]{3,2,1,0:T(8,128)S(1)}, f32[12,3,32,128]{3,2,1,0:T(8,128)S(1)}, f32[12,3,40,128]{3,2,1,0:T(8,128)S(1)}, f32[12,3,40,128]{3,2,1,0:T(8,128)S(1)}, f32[6,4,48,128]{3,2,1,0:T(8,128)S(1)}) custom-call(f32[12,32,384]{2,1,0:T(8,128)} %t_in.1, f32[12,32,384]{2,1,0:T(8,128)} %s_in.1, f32[12,32,384]{2,1,0:T(8,128)} %u_in.1, ...), custom_call_target="tpu_custom_call" | custom-call | tf_op jit(solution)/shard_map/pallas_call | solution.py:682
  18.2 2.1 %shard_map.145 = (f32[12,32,384]{2,1,0:T(8,128)}, f32[12,32,384]{2,1,0:T(8,128)}, f32[12,32,384]{2,1,0:T(8,128)}, f32[12,32,384]{2,1,0:T(8,128)}, f32[32,384]{1,...) custom-call(f32[12,3,32,128]{3,2,1,0:T(8,128)S(1)} %get-tuple-element.12.t, ...), custom_call_target="tpu_custom_call" | custom-call | tf_op jit(solution)/shard_map/pallas_call | solution.py:705

commit v3 on v2

--- a/solution.py
+++ b/solution.py
@@ -93,7 +93,8 @@
     t_out, s_out, u_out, v_out, flat_out,
     tr, sr, ur, vr, tm, sm, um, vm, pm, wu, ev, xt, xs, yt, ys, ratio,
     zt, mt, wi, bi, de, hue, hve, flat, fu_ref, fv_ref,
-    strip0, fe0, fw0, strip1, fe1, fw1, strip2, fe2, fw2, mend, edge_b, acc,
+    strip0, fe0, fw0, strip_a, fe_a, fw_a, strip_b, fe_b, fw_b, strip_c, fe_c,
+    strip2, fe2, fw2, mend, edge_b, acc, pn,
     load_sem, send1, recv1, send2, recv2,
 ):
     levels, nt, rows, _ = t_out.shape
@@ -141,10 +142,10 @@
 
     ld_wi = load(lambda s: wi_in.at[:, s], lambda c: wi.at[c])
     ld_bi = load(lambda s: bi_in.at[:, s], lambda c: bi.at[c])
+    ld_u = load(lambda s: u_in.at[:, :, s], lambda c: ur.at[:, c, own, :])
+    ld_v = load(lambda s: v_in.at[:, :, s], lambda c: vr.at[:, c, own, :])
     ld_t = load(lambda s: t_in.at[:, :, s], lambda c: tr.at[:, c, own, :])
     ld_s = load(lambda s: s_in.at[:, :, s], lambda c: sr.at[:, c, own, :])
-    ld_u = load(lambda s: u_in.at[:, :, s], lambda c: ur.at[:, c, own, :])
-    ld_v = load(lambda s: v_in.at[:, :, s], lambda c: vr.at[:, c, own, :])
     ld_e = load(lambda s: eta_in.at[:, s], lambda c: flat.at[0, c, own, :])
     ld_z = load(lambda s: zt_in.at[:, s], lambda c: zt.at[c])
     ld_m = load(lambda s: mt_in.at[:, s], lambda c: mt.at[c])
@@ -157,10 +158,8 @@
     def clear(first):
         beyond = slice(first, first + SUB)
         de[:, beyond, :] = jnp.zeros((nt + 1, SUB, LANES), F32)
-        for ref in (fe0, fw0, fe2, fw2):
+        for ref in (fe0, fw0, fe_b, fw_b, fe2, fw2):
             ref[beyond, :] = jnp.zeros((SUB, LANES), F32)
-        for ref in (fe1, fw1):
-            ref[:, beyond, :] = jnp.zeros((2, SUB, LANES), F32)
         for f in range(FLAT):
             flat[f, :, beyond, :] = jnp.zeros((nt, SUB, LANES), F32)
 
@@ -232,10 +231,16 @@
         return ref.at[0:nt, pl.ds(first, n), :]
 
     depth_up, depth_down = [rows_up(de, 2, plane_rows)], [rows_down(de, 2, plane_rows)]
-    field_up = [rows_up(r, n, cube_rows) for r, n in ((tr, 2), (sr, 2), (ur, 1), (vr, 1))]
-    field_down = [rows_down(r, n, cube_rows) for r, n in ((tr, 2), (sr, 2), (ur, 1), (vr, 1))]
-
-    def strips(cp, strip, fe, fw, at, n):
+    flow_up = [rows_up(r, 1, cube_rows) for r in (ur, vr)]
+    flow_down = [rows_down(r, 1, cube_rows) for r in (ur, vr)]
+    tracer_up = [rows_up(r, 2, cube_rows) for r in (tr, sr)]
+    tracer_down = [rows_down(r, 2, cube_rows) for r in (tr, sr)]
+    press_down = [cp(cube_rows(pm, SUB, 1), cube_rows(pn, 0, 1), lon, sth)]
+
+    def strips(cp, strip, fe, fw, n):
+        def at(ref, first, size):
+            return ref.at[pl.ds(first, size), :]
+
         along = [cp(at(strip, 0, rows), at(fe, SUB, rows), wst, lat),
                  cp(at(strip, 0, rows), at(fw, SUB, rows), est, lat)]
         up = [cp(at(strip, rows - n, n), at(fe, SUB - n, n), wst, nth),
@@ -245,9 +250,12 @@
         return along, up, down
 
     along0, corner_up0, corner_down0 = strips(
-        cp, strip0, fe0, fw0, lambda r, a, n: r.at[pl.ds(a, n), :], 2)
-    along1, corner_up1, corner_down1 = strips(
-        cp, strip1, fe1, fw1, lambda r, a, n: r.at[:, pl.ds(a, n), :], 2)
+        cp, strip0, fe0, fw0, 2)
+    along_b = [cp(strip_b, fe_b.at[own, :], wst, lat), cp(strip_b, fw_b.at[own, :], est, lat)]
+    corner_up_b = [cp(strip_b.at[pl.ds(rows - 1, 1), :], fe_b.at[pl.ds(SUB - 1, 1), :], wst, nth)]
+    corner_down_b = [cp(strip_b.at[pl.ds(0, 1), :], fw_b.at[pl.ds(end, 1), :], est, sth)]
+    along_a = [cp(strip_a, fe_a, wst, lat), cp(strip_a, fw_a, est, lat)]
+    along_c = [cp(strip_c, fe_c, wst, lat)]
 
     lane = lane_of((SUB, LANES))
     tall = lane_of((rows, LANES))
@@ -283,20 +291,23 @@
     for c in along0:
         c.start()
     start_ns(depth_up + corner_up0, depth_down + corner_down0)
-    for n, group in enumerate((ld_t, ld_s, ld_u, ld_v)):
+    for n, group in enumerate((ld_u, ld_v)):
         arrived(group)
-        start_ns(field_up[n:n + 1], field_down[n:n + 1])
+        start_ns(flow_up[n:n + 1], flow_down[n:n + 1])
+
+    place = lax.shift_right_logical(tall, 2)
+    group = jnp.zeros((rows, LANES), F32)
+    for k in range(levels):
+        for n, ref in enumerate((ur, vr)):
+            group = jnp.where(place == 2 * k + n, edge(ref[k, 0, own, :], ref[k, nt - 1, own, :], 2 * k + n), group)
+    strip_b[...] = group
+    for c in along_b:
+        c.start()
+    start_ns(corner_up_b, corner_down_b)
 
     HALF = 0.5 * GRAVITY_FACTOR * TIME_STEP
-
-    def pressure(t, s, total):
-        h = (HALF * HALINE_COEF) * s - (HALF * THERMAL_COEF) * t
-        p = total + h
-        return p, p + h
-
-    place = lax.shift_right_logical(tall, 2)
-    group_a = jnp.zeros((rows, LANES), F32)
-    group_b = jnp.zeros((rows, LANES), F32)
+    arrived(ld_t, ld_s)
+    group = jnp.zeros((rows, LANES), F32)
     total = jnp.zeros((nt, rows, LANES), F32)
     for k in range(levels):
         wet = de[0:nt, own, :] > k
@@ -304,48 +315,51 @@
         s = jnp.where(wet, sr[k, :, own, :], 0.0)
         tm[k, :, own, :] = t
         sm[k, :, own, :] = s
-        p, total = pressure(t, s, total)
+        h = (HALF * HALINE_COEF) * s - (HALF * THERMAL_COEF) * t
+        p = total + h
+        total = p + h
         pm[k, :, own, :] = p
-        group_a = jnp.where(place == 2 * k, edge(t[0], t[nt - 1], 2 * k), group_a)
-        group_a = jnp.where(place == 2 * k + 1, edge(s[0], s[nt - 1], 2 * k + 1), group_a)
-        group_b = jnp.where(place == 2 * k, edge(ur[k, 0, own, :], ur[k, nt - 1, own, :], 2 * k), group_b)
-        group_b = jnp.where(place == 2 * k + 1, edge(vr[k, 0, own, :], vr[k, nt - 1, own, :], 2 * k + 1), group_b)
-        group_b = jnp.where(tall == 8 * k + 7, pltpu.roll(p[0], 8 * k + 7, 1), group_b)
-    strip1[0] = group_a
-    strip1[1] = group_b
-    for c in along1:
+        group = jnp.where(tall == 8 * k + 1, pltpu.roll(p[0], 8 * k + 1, 1), group)
+    strip_c[...] = group
+    start_ns([], press_down)
+    for c in along_c:
         c.start()
-    start_ns(corner_up1, corner_down1)
+    start_ns(tracer_up, tracer_down)
+    group = jnp.zeros((rows, LANES), F32)
+    for k in range(levels):
+        for n, ref in enumerate((tm, sm)):
+            group = jnp.where(place == 2 * k + n, edge(ref[k, 0, own, :], ref[k, nt - 1, own, :], 2 * k + n), group)
+    strip_a[...] = group
+    for c in along_a:
+        c.start()
     arrived(ld_e, ld_z, ld_m)
     flat[5, :, own, :] = depth
 
+    def faces(first, last):
+        for r in range(first, last, SUB):
+            d = de[:, r:r + SUB, :]
+            hue[:, r:r + SUB, :] = jnp.minimum(d, east_all(d, lane))
+            hve[:, r:r + SUB, :] = jnp.minimum(d, de[:, r + 1:r + SUB + 1, :])
+
     for c in along0:
         c.wait_recv()
-    recv_ns(depth_up + corner_up0, depth_down + corner_down0)
-    high = lane_of((end + SUB, LANES))
-    pair = (high & 3) >= 2
-    de[nt, 0:end + SUB, :] = pltpu.roll(jnp.where(pair, fe0[...], fw0[...]), LANES - 2, 1)
-    for r in range(0, end + SUB, SUB):
-        d = de[:, r:r + SUB, :]
-        hue[:, r:r + SUB, :] = jnp.minimum(d, east_all(d, lane))
-        hve[:, r:r + SUB, :] = jnp.minimum(d, de[:, r + 1:r + SUB + 1, :])
+    recv_ns(depth_up, depth_down)
+    de[nt, own, :] = pltpu.roll(jnp.where((tall & 3) >= 2, fe0[own, :], fw0[own, :]), LANES - 2, 1)
+    faces(SUB, end)
 
     MIX = TIME_STEP * MOMENTUM_DIFF
     KEEP = 1.0 - TIME_STEP * BOTTOM_DRAG - 4.0 * MIX
 
-    @pl.loop(0, levels)
-    def _(k):
-        kf = k.astype(F32)
-        um[k, :, own, :] = jnp.where(hue[0:nt, own, :] > kf, ur[k, :, own, :], 0.0)
-        vm[k, :, own, :] = jnp.where(hve[0:nt, own, :] > kf, vr[k, :, own, :], 0.0)
-
-    @pl.loop(0, levels)
-    def _(k):
+    def momentum(k, carry):
         kf = k.astype(F32)
         for at in range(SUB, end, SUB):
             here = slice(at, at + SUB)
-            wu[k, :, here, :] = west_in(um[k, :, here, :], lane)
-            ev[k, :, here, :] = east_in(vm[k, :, here, :], lane, 1)
+            u = jnp.where(hue[0:nt, here, :] > kf, ur[k, :, here, :], 0.0)
+            v = jnp.where(hve[0:nt, here, :] > kf, vr[k, :, here, :], 0.0)
+            um[k, :, here, :] = u
+            vm[k, :, here, :] = v
+            wu[k, :, here, :] = west_in(u, lane)
+            ev[k, :, here, :] = east_in(v, lane, 1)
         for r in range(nr):
             at = SUB + SUB * r
             here, above, below = slice(at, at + SUB), slice(at + 1, at + SUB + 1), slice(at - 1, at + SUB - 1)
@@ -365,7 +379,9 @@
             v_out[k, :, out, :] = vt
             for n, x in enumerate((u, v, ut, vt)):
                 acc[n, :, out, :] += x
-
+        return carry
+
+    step_loop(0, levels, 2, momentum, 0)
     wind_u = jnp.where(hue[0:nt, own, :] > 0.0, (TIME_STEP * WIND_FACTOR) * zt[...], 0.0)
     wind_v = jnp.where(hve[0:nt, own, :] > 0.0, (TIME_STEP * WIND_FACTOR) * mt[...], 0.0)
     u_out[0, :, 0:rows, :] += wind_u
@@ -375,9 +391,14 @@
     flat[3, :, own, :] = acc[2] - acc[0] + wind_u
     flat[4, :, own, :] = acc[3] - acc[1] + wind_v
 
-    for c in along1:
+    recv_ns(corner_up0, corner_down0)
+    for out in (slice(0, SUB), slice(end, end + SUB)):
+        de[nt, out, :] = pltpu.roll(jnp.where((lane & 3) >= 2, fe0[out, :], fw0[out, :]), LANES - 2, 1)
+    faces(0, SUB)
+    faces(end - SUB, end + SUB)
+    for c in along_b + along_c:
         c.wait_recv()
-    recv_ns(corner_up1, corner_down1)
+    recv_ns(corner_up_b, corner_down_b)
     level = lax.shift_right_logical(tall, 3).astype(F32)
 
     def by_lane(at, one, two, five, six):
@@ -390,14 +411,13 @@
     for r in range(0, end + SUB, SUB):
         here = slice(r, r + SUB)
         limit = by_lane(lane & 7, *(column(ref, nt, at, here, SUB) for ref in (hue, hve) for at in (LAST, 0)))
-        limit = jnp.where((lane & 7) == 7, float(levels), limit)
-        x = jnp.where((lane & 3) >= 2, fe1[1, here, :], fw1[1, here, :])
+        x = jnp.where((lane & 3) >= 2, fe_b[here, :], fw_b[here, :])
         edge_b[here, :] = jnp.where(limit > lax.shift_right_logical(lane, 3).astype(F32), x, 0.0)
     x = edge_b[own, :]
     spot = tall & 7
     near = jnp.where((spot & 1) == 1, pltpu.roll(x, LAST, 1), pltpu.roll(x, 1, 1))
     above, below = slice(SUB + 1, end + 1), slice(SUB - 1, end - 1)
-    turn_u = fu_ref[...].reshape(rows, LANES) * pltpu.roll(x + edge_b[below, :], LANES - 5, 1) - pltpu.roll(x, LANES - 6, 1)
+    turn_u = fu_ref[...].reshape(rows, LANES) * pltpu.roll(x + edge_b[below, :], LANES - 5, 1) - fe_c[...]
     turn_v = fv_ref[...].reshape(rows, LANES) * pltpu.roll(x + edge_b[above, :], 5, 1)
     extra = MIX * near + jnp.where(spot == 1, turn_u, 0.0) - jnp.where(spot == 6, turn_v, 0.0)
     limit = by_lane(spot, column(hue, nt - 1, LAST), column(hue, 0, 0), column(hve, nt - 1, LAST), column(hve, 0, 0))
@@ -416,29 +436,20 @@
         flat[f, 0, own, :] += jnp.where(tall == 0, d, 0.0)
         flat[f, nt - 1, own, :] += jnp.where(tall == LAST, d, 0.0)
 
-    recv_ns(field_up, field_down)
+    recv_ns(flow_up, flow_down)
+    recv_ns([], press_down)
     top = lax.broadcasted_iota(jnp.int32, (SUB, LANES), 0) == 0
 
     def far_rows(k, carry):
-        total, nu, nv, su, sv = carry
+        nu, nv, su, sv = carry
         kf = k.astype(F32)
-        for a in (0, end):
-            out = slice(a, a + SUB)
-            wet = de[0:nt, out, :] > kf
-            tm[k, :, out, :] = jnp.where(wet, tr[k, :, out, :], 0.0)
-            sm[k, :, out, :] = jnp.where(wet, sr[k, :, out, :], 0.0)
-        out = slice(0, SUB)
-        vm[k, :, out, :] = jnp.where(hve[0:nt, out, :] > kf, vr[k, :, out, :], 0.0)
-
         out = slice(end, end + SUB)
-        wet = de[0:nt, out, :] > kf
-        p, total = pressure(jnp.where(wet, tr[k, :, out, :], 0.0), jnp.where(wet, sr[k, :, out, :], 0.0), total)
         u = jnp.where(hue[0:nt, out, :] > kf, ur[k, :, out, :], 0.0)
         v = jnp.where(hve[0:nt, out, :] > kf, vr[k, :, out, :], 0.0)
         edge_row = slice(end - 1, end + SUB - 1)
         du = jnp.where(top & (hue[0:nt, edge_row, :] > kf), MIX * u, 0.0)
         dv = jnp.where(top & (hve[0:nt, edge_row, :] > kf),
-                       MIX * v - fv_north * (u + west_in(u, lane)) - p, 0.0)
+                       MIX * v - fv_north * (u + west_in(u, lane)) - pn[k], 0.0)
         row = slice(rows - 1, rows + SUB - 1)
         u_out[k, :, row, :] += du
         v_out[k, :, row, :] += dv
@@ -453,9 +464,9 @@
         dv = jnp.where(top & (hve[0:nt, edge_row, :] > kf), MIX * v, 0.0)
         u_out[k, :, 0:SUB, :] += du
         v_out[k, :, 0:SUB, :] += dv
-        return total, nu, nv, su + du, sv + dv
-
-    _, nu, nv, su, sv = step_loop(0, levels, 2, far_rows, (zero,) * 5)
+        return nu, nv, su + du, sv + dv
+
+    nu, nv, su, sv = step_loop(0, levels, 2, far_rows, (zero,) * 4)
     for f, north, south in ((3, nu, su), (4, nv, sv)):
         flat[f, :, SUB:2 * SUB, :] += south
         flat[f, :, end - SUB:end, :] += pltpu.roll(north, SUB - 1, 1)
@@ -470,16 +481,29 @@
     flat_up = [cp(cube_rows(flat, end - NSUB, NSUB), cube_rows(flat, SUB - NSUB, NSUB), lon, nth)]
     flat_down = [cp(cube_rows(flat, SUB, NSUB), cube_rows(flat, end, NSUB), lon, sth)]
     along2, corner_up2, corner_down2 = strips(
-        cp, strip2, fe2, fw2, lambda r, a, n: r.at[pl.ds(a, n), :], NSUB)
+        cp, strip2, fe2, fw2, NSUB)
     start_ns(flat_up, flat_down)
     for c in along2:
         c.start()
     start_ns(corner_up2, corner_down2)
 
+    recv_ns(tracer_up, tracer_down)
+
+    def tracer_rows(k, carry):
+        kf = k.astype(F32)
+        for a in (0, end):
+            out = slice(a, a + SUB)
+            wet = de[0:nt, out, :] > kf
+            tm[k, :, out, :] = jnp.where(wet, tr[k, :, out, :], 0.0)
+            sm[k, :, out, :] = jnp.where(wet, sr[k, :, out, :], 0.0)
+        vm[k, :, 0:SUB, :] = jnp.where(hve[0:nt, 0:SUB, :] > kf, vr[k, :, 0:SUB, :], 0.0)
+        return carry
+
+    step_loop(0, levels, 2, tracer_rows, 0)
+
     starts = list(range(SUB - 1, end - SUB, SUB)) + [end - SUB]
 
-    @pl.loop(0, levels)
-    def _(k):
+    def fluxes(k, carry):
         kf = k.astype(F32)
         for r in range(SUB, end, SUB):
             here = slice(r, r + SUB)
@@ -488,7 +512,7 @@
                 c = ref[k, :, here, :]
                 fx = (w0 * c + w1 * east_in(c, lane, 1)
                       - w2 * east_in(c, lane, 2) + w3 * west_in(c, lane))
-                to[k, :, r - SUB:r, :] = c - (fx - west_in(fx, lane))
+                to[k, :, r - SUB:r, :] = fx
         for a in starts:
             here = slice(a, a + SUB)
             w0, w1, w2, w3 = face_weights(vm[k, :, here, :], hve[0:nt, here, :] > kf)
@@ -496,6 +520,11 @@
                 to[k, :, here, :] = (
                     w0 * ref[k, :, here, :] + w1 * ref[k, :, a + 1:a + SUB + 1, :]
                     - w2 * ref[k, :, a + 2:a + SUB + 2, :] + w3 * ref[k, :, a - 1:a + SUB - 1, :])
+        return carry
+
+    step_loop(0, levels, 1, fluxes, 0)
+    for c in along_a:
+        c.wait_recv()
 
     q = tall & 3
 
@@ -504,15 +533,15 @@
         opening = limit > level
         return face_weights(jnp.where(opening, x, 0.0), opening)
 
-    mine = strip1[0]
-    a = jnp.where(q < 2, mine, fe1[0, own, :])
-    b = jnp.where(q < 2, fw1[0, own, :], mine)
-    _, w1, w2, w3 = speeds(strip1[1], jnp.where(
+    mine = strip_a[...]
+    a = jnp.where(q < 2, mine, fe_a[...])
+    b = jnp.where(q < 2, fw_a[...], mine)
+    _, w1, w2, w3 = speeds(strip_b[...], jnp.where(
         q == 0, column(hue, nt - 1, LANES - 2), jnp.where(q == 1, column(hue, nt - 1, LAST), column(hue, 0, 0))))
     b_west = pltpu.roll(b, 1, 1)
     flux = jnp.where(q == 1, w1 * pltpu.roll(a, LANES - 1, 1), 0.0) - w2 * pltpu.roll(a, LANES - 2, 1)
     flux = jnp.where(q < 2, flux, jnp.where(q == 2, w3 * b_west, 0.0))
-    w0, w1, w2, w3 = speeds(fw1[1, own, :], column(hue, nt, LAST))
+    w0, w1, w2, w3 = speeds(fw_b[own, :], column(hue, nt, LAST))
     first = w0 * b + w1 * pltpu.roll(b, LANES - 1, 1) - w2 * pltpu.roll(b, LANES - 2, 1) + w3 * b_west
     mend[...] = flux - pltpu.roll(jnp.where(q == 1, first, flux), 1, 1)
 
@@ -523,6 +552,7 @@
         return jnp.concatenate([first, x[1:-1], last], axis=0)
 
     span = 2 * SUB if rows % (2 * SUB) == 0 else SUB
+    long = lane_of((span, LANES))
     DIFF = TIME_STEP * STABILITY_FACTOR * BACKGROUND_MIX
     BASE = TIME_STEP * (BACKGROUND_MIX + CONVECTIVE_MIX)
     for r in range(0, rows, span):
@@ -530,8 +560,10 @@
         here, below = slice(SUB + r, SUB + r + span), slice(SUB + r - 1, SUB + r + span - 1)
 
         def star(k):
-            t = xt[k, :, out, :] - (yt[k, :, here, :] - yt[k, :, below, :])
-            s = xs[k, :, out, :] - (ys[k, :, here, :] - ys[k, :, below, :])
+            fx = xt[k, :, out, :]
+            t = tm[k, :, here, :] - (fx - west_in(fx, long)) - (yt[k, :, here, :] - yt[k, :, below, :])
+            fx = xs[k, :, out, :]
+            s = sm[k, :, here, :] - (fx - west_in(fx, long)) - (ys[k, :, here, :] - ys[k, :, below, :])
             t = mended(t, pltpu.roll(mend[out, :], LANES - 2 - 8 * k, 1))
             s = mended(s, pltpu.roll(mend[out, :], LANES - 6 - 8 * k, 1))
             return t, s, HALINE_COEF * s - THERMAL_COEF * t
@@ -571,6 +603,10 @@
 
         lax.fori_loop(0, levels - 1, backward, (t, s))
 
+    for c in along0 + along_a + along_b + along_c:
+        c.wait_send()
+    sent_ns(depth_up + corner_up0 + flow_up + tracer_up + corner_up_b,
+            depth_down + corner_down0 + flow_down + tracer_down + corner_down_b + press_down)
     recv_ns(flat_up, flat_down)
     for c in along2:
         c.wait_recv()
@@ -583,10 +619,9 @@
         flat_out[f, nt, 0:count] = pltpu.roll(halo, LANES - 8 * f - 4, 1)
     flat_out[5, :, count:, :] = jnp.zeros((nt + 1, SUB, LANES), F32)
 
-    for c in along0 + along1 + along2:
+    for c in along2:
         c.wait_send()
-    sent_ns(depth_up + corner_up0 + field_up + corner_up1 + flat_up + corner_up2,
-            depth_down + corner_down0 + field_down + corner_down1 + flat_down + corner_down2)
+    sent_ns(flat_up + corner_up2, flat_down + corner_down2)
 
 
 def tail(
@@ -677,7 +712,7 @@
     raw = vmem(levels, nt, erows, LANES)
     own = vmem(levels, nt, rows, LANES)
     ints = pltpu.VMEM((nt, rows, LANES), jnp.int32)
-    n1, n2 = 2 + 8 + 6 + 6, 2 + 6
+    n1, n2 = 2 + 8 + 1 + 6 + 4 + 3, 2 + 6
     cube = (levels, nt, rows, LANES)
     parts = pl.pallas_call(
         functools.partial(kernel, rows * lax.axis_size("lat")),
@@ -691,9 +726,11 @@
             + [vmem(FLAT, nt, erows, LANES)]
             + [vmem(rows // SUB, SUB, LANES)] * 2
             + [vmem(rows, LANES), vmem(erows, LANES), vmem(erows, LANES)]
-            + [vmem(2, rows, LANES), vmem(2, erows, LANES), vmem(2, erows, LANES)]
+            + [vmem(rows, LANES)] * 3
+            + [vmem(rows, LANES), vmem(erows, LANES), vmem(erows, LANES)]
+            + [vmem(rows, LANES)] * 2
             + [vmem(rows, LANES), vmem(erows, LANES), vmem(erows, LANES), vmem(rows, LANES)]
-            + [vmem(erows, LANES), vmem(4, nt, rows, LANES)]
+            + [vmem(erows, LANES), vmem(4, nt, rows, LANES), vmem(levels, nt, SUB, LANES)]
             + [pltpu.SemaphoreType.DMA((9 * nt,))]
             + [pltpu.SemaphoreType.DMA((n1,))] * 2
             + [pltpu.SemaphoreType.DMA((n2,))] * 2

time: 20.5 us -> 19.4 us (0.946)
  Pallas kernels: 19.7 us -> 18.6 us
    pallas_call x1, Pallas kernels: 17.6 us -> 16.5 us  [body(): pl.pallas_call(functools.partial(kernel, rows * lax.axis_size('lat')), ou...]
where the time goes in v3:
time: 19.4 us; the launch traced here: 19.2 us
  Pallas kernels  18.6 us (96%)
  between operations  0.64 us (3%)
    pallas_call x1, Pallas kernels, body(): pl.pallas_call(functools.partial(kernel, rows * lax.axis_size('lat')), ou...  16.5 us
    pallas_call x1, Pallas kernels, body(): pl.pallas_call(tail, out_shape=(pltpu.HBM(cube, F32),) * 4 + (pltpu.HBM(p...  2.1 us

profile of v3, /device:TPU:0, one launch (start us, length us, event | category | flops | bytes accessed | tf_op | source)
XLA Modules:
  0.0 19.2 jit_solution(15687128257922650721)
XLA Ops:
  0.6 16.5 %shard_map.144 = (f32[12,3,32,128]{3,2,1,0:T(8,128)S(1)}, f32[12,3,32,128]{3,2,1,0:T(8,128)S(1)}, f32[12,3,40,128]{3,2,1,0:T(8,128)S(1)}, f32[12,3,40,128]{3,2,1,0:T(8,128)S(1)}, f32[6,4,48,128]{3,2,1,0:T(8,128)S(1)}) custom-call(f32[12,32,384]{2,1,0:T(8,128)} %t_in.1, f32[12,32,384]{2,1,0:T(8,128)} %s_in.1, f32[12,32,384]{2,1,0:T(8,128)} %u_in.1, ...), custom_call_target="tpu_custom_call" | custom-call | tf_op jit(solution)/shard_map/pallas_call | solution.py:717
  17.1 2.1 %shard_map.145 = (f32[12,32,384]{2,1,0:T(8,128)}, f32[12,32,384]{2,1,0:T(8,128)}, f32[12,32,384]{2,1,0:T(8,128)}, f32[12,32,384]{2,1,0:T(8,128)}, f32[32,384]{1,...) custom-call(f32[12,3,32,128]{3,2,1,0:T(8,128)S(1)} %get-tuple-element.12.t, ...), custom_call_target="tpu_custom_call" | custom-call | tf_op jit(solution)/shard_map/pallas_call | solution.py:742

commit v4 on v3

--- a/solution.py
+++ b/solution.py
@@ -340,6 +340,24 @@
             d = de[:, r:r + SUB, :]
             hue[:, r:r + SUB, :] = jnp.minimum(d, east_all(d, lane))
             hve[:, r:r + SUB, :] = jnp.minimum(d, de[:, r + 1:r + SUB + 1, :])
+
+    for r in range(SUB, end, SUB):
+        d = de[0:nt, r:r + SUB, :]
+        hue[0:nt, r:r + SUB, :] = jnp.minimum(d, east_in(d, lane, 1))
+
+    def east_fluxes(k, carry):
+        kf = k.astype(F32)
+        for r in range(SUB, end, SUB):
+            here = slice(r, r + SUB)
+            opening = hue[0:nt, here, :] > kf
+            w0, w1, w2, w3 = face_weights(jnp.where(opening, ur[k, :, here, :], 0.0), opening)
+            for ref, to in ((tm, xt), (sm, xs)):
+                c = ref[k, :, here, :]
+                to[k, :, r - SUB:r, :] = (w0 * c + w1 * east_in(c, lane, 1)
+                                          - w2 * east_in(c, lane, 2) + w3 * west_in(c, lane))
+        return carry
+
+    step_loop(0, levels, 1, east_fluxes, 0)
 
     for c in along0:
         c.wait_recv()
@@ -422,16 +440,10 @@
     extra = MIX * near + jnp.where(spot == 1, turn_u, 0.0) - jnp.where(spot == 6, turn_v, 0.0)
     limit = by_lane(spot, column(hue, nt - 1, LAST), column(hue, 0, 0), column(hve, nt - 1, LAST), column(hve, 0, 0))
     extra = jnp.where(limit > level, extra, 0.0)
-    total_u = jnp.zeros((rows, LANES), F32)
-    total_v = jnp.zeros((rows, LANES), F32)
+    total = jnp.zeros((rows, LANES), F32)
     for k in range(levels):
-        du = pltpu.roll(extra, LANES - 2 - 8 * k, 1)
-        dv = pltpu.roll(extra, LANES - 6 - 8 * k, 1)
-        for ref, d in ((u_out, du), (v_out, dv)):
-            ref[k, 0, 0:rows, :] += jnp.where(tall == 0, d, 0.0)
-            ref[k, nt - 1, 0:rows, :] += jnp.where(tall == LAST, d, 0.0)
-        total_u = total_u + du
-        total_v = total_v + dv
+        total = total + (pltpu.roll(extra, LANES - 8 * k, 1) if k else extra)
+    total_u, total_v = pltpu.roll(total, LANES - 2, 1), pltpu.roll(total, LANES - 6, 1)
     for f, d in ((3, total_u), (4, total_v)):
         flat[f, 0, own, :] += jnp.where(tall == 0, d, 0.0)
         flat[f, nt - 1, own, :] += jnp.where(tall == LAST, d, 0.0)
@@ -487,6 +499,13 @@
         c.start()
     start_ns(corner_up2, corner_down2)
 
+    for k in range(levels):
+        du = pltpu.roll(extra, LANES - 2 - 8 * k, 1)
+        dv = pltpu.roll(extra, LANES - 6 - 8 * k, 1)
+        for ref, d in ((u_out, du), (v_out, dv)):
+            ref[k, 0, 0:rows, :] += jnp.where(tall == 0, d, 0.0)
+            ref[k, nt - 1, 0:rows, :] += jnp.where(tall == LAST, d, 0.0)
+
     recv_ns(tracer_up, tracer_down)
 
     def tracer_rows(k, carry):
@@ -503,16 +522,8 @@
 
     starts = list(range(SUB - 1, end - SUB, SUB)) + [end - SUB]
 
-    def fluxes(k, carry):
+    def north_fluxes(k, carry):
         kf = k.astype(F32)
-        for r in range(SUB, end, SUB):
-            here = slice(r, r + SUB)
-            w0, w1, w2, w3 = face_weights(um[k, :, here, :], hue[0:nt, here, :] > kf)
-            for ref, to in ((tm, xt), (sm, xs)):
-                c = ref[k, :, here, :]
-                fx = (w0 * c + w1 * east_in(c, lane, 1)
-                      - w2 * east_in(c, lane, 2) + w3 * west_in(c, lane))
-                to[k, :, r - SUB:r, :] = fx
         for a in starts:
             here = slice(a, a + SUB)
             w0, w1, w2, w3 = face_weights(vm[k, :, here, :], hve[0:nt, here, :] > kf)
@@ -522,7 +533,7 @@
                     - w2 * ref[k, :, a + 2:a + SUB + 2, :] + w3 * ref[k, :, a - 1:a + SUB - 1, :])
         return carry
 
-    step_loop(0, levels, 1, fluxes, 0)
+    step_loop(0, levels, 1, north_fluxes, 0)
     for c in along_a:
         c.wait_recv()
 
@@ -536,10 +547,11 @@
     mine = strip_a[...]
     a = jnp.where(q < 2, mine, fe_a[...])
     b = jnp.where(q < 2, fw_a[...], mine)
-    _, w1, w2, w3 = speeds(strip_b[...], jnp.where(
+    w0, w1, w2, w3 = speeds(strip_b[...], jnp.where(
         q == 0, column(hue, nt - 1, LANES - 2), jnp.where(q == 1, column(hue, nt - 1, LAST), column(hue, 0, 0))))
     b_west = pltpu.roll(b, 1, 1)
-    flux = jnp.where(q == 1, w1 * pltpu.roll(a, LANES - 1, 1), 0.0) - w2 * pltpu.roll(a, LANES - 2, 1)
+    flux = (jnp.where(q == 1, w0 * a + w1 * pltpu.roll(a, LANES - 1, 1) + w3 * pltpu.roll(a, 1, 1), 0.0)
+            - w2 * pltpu.roll(a, LANES - 2, 1))
     flux = jnp.where(q < 2, flux, jnp.where(q == 2, w3 * b_west, 0.0))
     w0, w1, w2, w3 = speeds(fw_b[own, :], column(hue, nt, LAST))
     first = w0 * b + w1 * pltpu.roll(b, LANES - 1, 1) - w2 * pltpu.roll(b, LANES - 2, 1) + w3 * b_west

time: 19.4 us -> 18.5 us (0.954)
  Pallas kernels: 18.6 us -> 17.7 us
    pallas_call x1, Pallas kernels: 16.5 us -> 15.6 us  [body(): pl.pallas_call(functools.partial(kernel, rows * lax.axis_size('lat')), ou...]
where the time goes in v4:
time: 18.5 us; the launch traced here: 18.4 us
  Pallas kernels  17.7 us (96%)
  between operations  0.64 us (3%)
    pallas_call x1, Pallas kernels, body(): pl.pallas_call(functools.partial(kernel, rows * lax.axis_size('lat')), ou...  15.6 us
    pallas_call x1, Pallas kernels, body(): pl.pallas_call(tail, out_shape=(pltpu.HBM(cube, F32),) * 4 + (pltpu.HBM(p...  2.1 us

profile of v4, /device:TPU:0, one launch (start us, length us, event | category | flops | bytes accessed | tf_op | source)
XLA Modules:
  0.0 18.4 jit_solution(3615933420620505263)
XLA Ops:
  0.6 15.6 %shard_map.144 = (f32[12,3,32,128]{3,2,1,0:T(8,128)S(1)}, f32[12,3,32,128]{3,2,1,0:T(8,128)S(1)}, f32[12,3,40,128]{3,2,1,0:T(8,128)S(1)}, f32[12,3,40,128]{3,2,1,0:T(8,128)S(1)}, f32[6,4,48,128]{3,2,1,0:T(8,128)S(1)}) custom-call(f32[12,32,384]{2,1,0:T(8,128)} %t_in.1, f32[12,32,384]{2,1,0:T(8,128)} %s_in.1, f32[12,32,384]{2,1,0:T(8,128)} %u_in.1, ...), custom_call_target="tpu_custom_call" | custom-call | tf_op jit(solution)/shard_map/pallas_call | solution.py:729
  16.3 2.1 %shard_map.145 = (f32[12,32,384]{2,1,0:T(8,128)}, f32[12,32,384]{2,1,0:T(8,128)}, f32[12,32,384]{2,1,0:T(8,128)}, f32[12,32,384]{2,1,0:T(8,128)}, f32[32,384]{1,...) custom-call(f32[12,3,32,128]{3,2,1,0:T(8,128)S(1)} %get-tuple-element.12.t, ...), custom_call_target="tpu_custom_call" | custom-call | tf_op jit(solution)/shard_map/pallas_call | solution.py:754

commit v5 on v4

--- a/solution.py
+++ b/solution.py
@@ -27,6 +27,7 @@
 LANES = 128
 SUB = 8
 FLAT = 6
+EARLY = 12
 MESH = pl.DeviceIdType.MESH
 F32 = jnp.float32
 
@@ -71,7 +72,9 @@
 
 def east_in(x, lane, s):
     r = pltpu.roll(x, LANES - s, 2)
-    return jnp.where(lane < LANES - s, r, jnp.concatenate([r[1:], jnp.zeros_like(r[:1])], axis=0))
+    beyond = jnp.zeros_like(r[:1])
+    beyond = jnp.concatenate([r[1:], beyond], axis=0) if x.shape[0] > 1 else beyond
+    return jnp.where(lane < LANES - s, r, beyond)
 
 
 def west_in(x, lane):
@@ -91,7 +94,7 @@
     lat_total,
     t_in, s_in, u_in, v_in, eta_in, zt_in, mt_in, wi_in, bi_in,
     t_out, s_out, u_out, v_out, flat_out,
-    tr, sr, ur, vr, tm, sm, um, vm, pm, wu, ev, xt, xs, yt, ys, ratio,
+    tr, sr, ur, vr, tm, sm, um, vm, pm, wu, ev, xu, xv, px, huc, hvc, dz, xt, xs, yt, ys, ratio,
     zt, mt, wi, bi, de, hue, hve, flat, fu_ref, fv_ref,
     strip0, fe0, fw0, strip_a, fe_a, fw_a, strip_b, fe_b, fw_b, strip_c, fe_c,
     strip2, fe2, fw2, mend, edge_b, acc, pn,
@@ -100,6 +103,7 @@
     levels, nt, rows, _ = t_out.shape
     end = SUB + rows
     zero = jnp.zeros((nt, SUB, LANES), F32)
+    early = EARLY * levels // 12
     nr = rows // SUB
     lon, lat = lax.axis_index("lon"), lax.axis_index("lat")
     nlon, nlat = lax.axis_size("lon"), lax.axis_size("lat")
@@ -341,15 +345,18 @@
             hue[:, r:r + SUB, :] = jnp.minimum(d, east_all(d, lane))
             hve[:, r:r + SUB, :] = jnp.minimum(d, de[:, r + 1:r + SUB + 1, :])
 
+    dz[:, 0:rows, :] = depth
+    dz[:, rows:, :] = zero
     for r in range(SUB, end, SUB):
-        d = de[0:nt, r:r + SUB, :]
-        hue[0:nt, r:r + SUB, :] = jnp.minimum(d, east_in(d, lane, 1))
+        d = dz[:, r - SUB:r, :]
+        huc[:, r - SUB:r, :] = jnp.minimum(d, east_in(d, lane, 1))
+        hvc[:, r - SUB:r, :] = jnp.minimum(d, dz[:, r - SUB + 1:r + 1, :])
 
     def east_fluxes(k, carry):
         kf = k.astype(F32)
         for r in range(SUB, end, SUB):
             here = slice(r, r + SUB)
-            opening = hue[0:nt, here, :] > kf
+            opening = huc[:, r - SUB:r, :] > kf
             w0, w1, w2, w3 = face_weights(jnp.where(opening, ur[k, :, here, :], 0.0), opening)
             for ref, to in ((tm, xt), (sm, xs)):
                 c = ref[k, :, here, :]
@@ -357,7 +364,59 @@
                                           - w2 * east_in(c, lane, 2) + w3 * west_in(c, lane))
         return carry
 
-    step_loop(0, levels, 1, east_fluxes, 0)
+    MIX = TIME_STEP * MOMENTUM_DIFF
+    KEEP = 1.0 - TIME_STEP * BOTTOM_DRAG - 4.0 * MIX
+
+    def sides(k, carry):
+        kf = k.astype(F32)
+        for r in range(0, rows, SUB):
+            here, out = slice(SUB + r, 2 * SUB + r), slice(r, r + SUB)
+            u = jnp.where(huc[:, out, :] > kf, ur[k, :, here, :], 0.0)
+            v = jnp.where(hvc[:, out, :] > kf, vr[k, :, here, :], 0.0)
+            w, e = west_in(u, lane), east_in(v, lane, 1)
+            um[k, :, here, :] = u
+            vm[k, :, here, :] = v
+            wu[k, :, here, :] = w
+            ev[k, :, here, :] = e
+            xu[k, :, out, :] = east_in(u, lane, 1) + w
+            xv[k, :, out, :] = west_in(v, lane) + e
+            p = pm[k, :, here, :]
+            px[k, :, out, :] = east_in(p, lane, 1) - p
+        return carry
+
+    def momentum(k, r, tiles):
+        kf = k.astype(F32)
+        at = SUB + SUB * r
+        here, above, below = slice(at, at + SUB), slice(at + 1, at + SUB + 1), slice(at - 1, at + SUB - 1)
+        out = slice(SUB * r, SUB * r + SUB)
+        u, un, w = um[k, tiles, here, :], um[k, tiles, above, :], wu[k, tiles, here, :]
+        v, vs, e = vm[k, tiles, here, :], vm[k, tiles, below, :], ev[k, tiles, here, :]
+        around_u = xu[k, tiles, out, :] + (un + um[k, tiles, below, :])
+        around_v = xv[k, tiles, out, :] + (vs + vm[k, tiles, above, :])
+        vbar = (v + vs) + (e + ev[k, tiles, below, :])
+        ubar = (u + un) + (w + wu[k, tiles, above, :])
+        py = pm[k, tiles, above, :] - pm[k, tiles, here, :]
+        ut = KEEP * u + MIX * around_u + fu_ref[r] * vbar - px[k, tiles, out, :]
+        vt = KEEP * v + MIX * around_v - fv_ref[r] * ubar - py
+        ut = jnp.where(hue[tiles, here, :] > kf, ut, 0.0)
+        vt = jnp.where(hve[tiles, here, :] > kf, vt, 0.0)
+        u_out[k, tiles, out, :] = ut
+        v_out[k, tiles, out, :] = vt
+        for n, x in enumerate((u, v, ut, vt)):
+            acc[n, tiles, out, :] += x
+
+    inner, rim = slice(0, nt - 1), slice(nt - 1, nt)
+    hue[0:nt, own, :] = huc[...]
+    hve[0:nt, own, :] = hvc[...]
+    step_loop(0, levels, 6, sides, 0)
+
+    def inside(k, carry):
+        for r in range(nr - 1):
+            momentum(k, r, inner)
+        return carry
+
+    step_loop(0, levels, 2, inside, 0)
+    step_loop(0, early, 4, east_fluxes, 0)
 
     for c in along0:
         c.wait_recv()
@@ -365,41 +424,28 @@
     de[nt, own, :] = pltpu.roll(jnp.where((tall & 3) >= 2, fe0[own, :], fw0[own, :]), LANES - 2, 1)
     faces(SUB, end)
 
-    MIX = TIME_STEP * MOMENTUM_DIFF
-    KEEP = 1.0 - TIME_STEP * BOTTOM_DRAG - 4.0 * MIX
-
-    def momentum(k, carry):
+
+    def last_sides(k, carry):
         kf = k.astype(F32)
-        for at in range(SUB, end, SUB):
-            here = slice(at, at + SUB)
-            u = jnp.where(hue[0:nt, here, :] > kf, ur[k, :, here, :], 0.0)
-            v = jnp.where(hve[0:nt, here, :] > kf, vr[k, :, here, :], 0.0)
-            um[k, :, here, :] = u
-            vm[k, :, here, :] = v
-            wu[k, :, here, :] = west_in(u, lane)
-            ev[k, :, here, :] = east_in(v, lane, 1)
-        for r in range(nr):
-            at = SUB + SUB * r
-            here, above, below = slice(at, at + SUB), slice(at + 1, at + SUB + 1), slice(at - 1, at + SUB - 1)
-            out = slice(SUB * r, SUB * r + SUB)
-            u, un, w = um[k, :, here, :], um[k, :, above, :], wu[k, :, here, :]
-            v, vs, e = vm[k, :, here, :], vm[k, :, below, :], ev[k, :, here, :]
-            p = pm[k, :, here, :]
-            around_u = (east_in(u, lane, 1) + w) + (un + um[k, :, below, :])
-            around_v = (west_in(v, lane) + e) + (vs + vm[k, :, above, :])
-            vbar = (v + vs) + (e + ev[k, :, below, :])
-            ubar = (u + un) + (w + wu[k, :, above, :])
-            ut = KEEP * u + MIX * around_u + fu_ref[r] * vbar - (east_in(p, lane, 1) - p)
-            vt = KEEP * v + MIX * around_v - fv_ref[r] * ubar - (pm[k, :, above, :] - p)
-            ut = jnp.where(hue[0:nt, here, :] > kf, ut, 0.0)
-            vt = jnp.where(hve[0:nt, here, :] > kf, vt, 0.0)
-            u_out[k, :, out, :] = ut
-            v_out[k, :, out, :] = vt
-            for n, x in enumerate((u, v, ut, vt)):
-                acc[n, :, out, :] += x
+        u = jnp.where(hue[rim, own, :] > kf, ur[k, rim, own, :], 0.0)
+        um[k, rim, own, :] = u
+        xu[k, rim, :, :] = east_in(u, tall, 1) + wu[k, rim, own, :]
+        here, out = slice(end - SUB, end), slice(rows - SUB, rows)
+        v = jnp.where(hve[0:nt, here, :] > kf, vr[k, :, here, :], 0.0)
+        e = east_in(v, lane, 1)
+        vm[k, :, here, :] = v
+        ev[k, :, here, :] = e
+        xv[k, :, out, :] = west_in(v, lane) + e
         return carry
 
-    step_loop(0, levels, 2, momentum, 0)
+    def outside(k, carry):
+        for r in range(nr - 1):
+            momentum(k, r, rim)
+        momentum(k, nr - 1, slice(0, nt))
+        return carry
+
+    step_loop(0, levels, 6, last_sides, 0)
+    step_loop(0, levels, 4, outside, 0)
     wind_u = jnp.where(hue[0:nt, own, :] > 0.0, (TIME_STEP * WIND_FACTOR) * zt[...], 0.0)
     wind_v = jnp.where(hve[0:nt, own, :] > 0.0, (TIME_STEP * WIND_FACTOR) * mt[...], 0.0)
     u_out[0, :, 0:rows, :] += wind_u
@@ -478,7 +524,7 @@
         v_out[k, :, 0:SUB, :] += dv
         return nu, nv, su + du, sv + dv
 
-    nu, nv, su, sv = step_loop(0, levels, 2, far_rows, (zero,) * 4)
+    nu, nv, su, sv = step_loop(0, levels, 4, far_rows, (zero,) * 4)
     for f, north, south in ((3, nu, su), (4, nv, sv)):
         flat[f, :, SUB:2 * SUB, :] += south
         flat[f, :, end - SUB:end, :] += pltpu.roll(north, SUB - 1, 1)
@@ -533,6 +579,7 @@
                     - w2 * ref[k, :, a + 2:a + SUB + 2, :] + w3 * ref[k, :, a - 1:a + SUB - 1, :])
         return carry
 
+    step_loop(early, levels, 4, east_fluxes, 0)
     step_loop(0, levels, 1, north_fluxes, 0)
     for c in along_a:
         c.wait_recv()
@@ -597,7 +644,7 @@
 
         zero = jnp.zeros((nt, span, LANES), F32)
         carry = star(0) + (zero + 1.0, zero, zero)
-        t, s, _, lower, qt, qs = lax.fori_loop(1, levels, forward, carry)
+        t, s, _, lower, qt, qs = step_loop(1, levels, 2, forward, carry)
         w = 1.0 / lower
         t, s = (t + qt) * w, (s + qs) * w
         t_out[levels - 1, :, out, :] = t
@@ -613,7 +660,7 @@
             s_out[k, :, out, :] = s
             return t, s
 
-        lax.fori_loop(0, levels - 1, backward, (t, s))
+        step_loop(0, levels - 1, 1, backward, (t, s))
 
     for c in along0 + along_a + along_b + along_c:
         c.wait_send()
@@ -732,7 +779,8 @@
         in_specs=[far] * 9,
         out_specs=(block,) * 5,
         scratch_shapes=(
-            [raw] * 11 + [own, own, raw, raw, own]
+            [raw] * 11 + [own] * 3 + [vmem(nt, rows, LANES)] * 2
+            + [vmem(nt, rows + SUB, LANES), own, own, raw, raw, own]
             + [vmem(nt, rows, LANES)] * 2 + [ints] * 2
             + [vmem(nt + 1, erows + SUB, LANES)] + [vmem(nt + 1, erows, LANES)] * 2
             + [vmem(FLAT, nt, erows, LANES)]

time: 18.5 us -> 17.2 us (0.930)
  Pallas kernels: 17.7 us -> 16.4 us
    pallas_call x1, Pallas kernels: 15.6 us -> 14.3 us  [body(): pl.pallas_call(functools.partial(kernel, rows * lax.axis_size('lat')), ou...]
where the time goes in v5:
time: 17.2 us; the launch traced here: 17.1 us
  Pallas kernels  16.4 us (95%)
  between operations  0.64 us (4%)
    pallas_call x1, Pallas kernels, body(): pl.pallas_call(functools.partial(kernel, rows * lax.axis_size('lat')), ou...  14.3 us
    pallas_call x1, Pallas kernels, body(): pl.pallas_call(tail, out_shape=(pltpu.HBM(cube, F32),) * 4 + (pltpu.HBM(p...  2.1 us

profile of v5, /device:TPU:0, one launch (start us, length us, event | category | flops | bytes accessed | tf_op | source)
XLA Modules:
  0.0 17.1 jit_solution(12340511032325768887)
XLA Ops:
  0.6 14.3 %shard_map.144 = (f32[12,3,32,128]{3,2,1,0:T(8,128)S(1)}, f32[12,3,32,128]{3,2,1,0:T(8,128)S(1)}, f32[12,3,40,128]{3,2,1,0:T(8,128)S(1)}, f32[12,3,40,128]{3,2,1,0:T(8,128)S(1)}, f32[6,4,48,128]{3,2,1,0:T(8,128)S(1)}) custom-call(f32[12,32,384]{2,1,0:T(8,128)} %t_in.1, f32[12,32,384]{2,1,0:T(8,128)} %s_in.1, f32[12,32,384]{2,1,0:T(8,128)} %u_in.1, ...), custom_call_target="tpu_custom_call" | custom-call | tf_op jit(solution)/shard_map/pallas_call | solution.py:776
  15.0 2.1 %shard_map.145 = (f32[12,32,384]{2,1,0:T(8,128)}, f32[12,32,384]{2,1,0:T(8,128)}, f32[12,32,384]{2,1,0:T(8,128)}, f32[12,32,384]{2,1,0:T(8,128)}, f32[32,384]{1,...) custom-call(f32[12,3,32,128]{3,2,1,0:T(8,128)S(1)} %get-tuple-element.12.t, ...), custom_call_target="tpu_custom_call" | custom-call | tf_op jit(solution)/shard_map/pallas_call | solution.py:802

commit v6 on v5

--- a/solution.py
+++ b/solution.py
@@ -27,7 +27,9 @@
 LANES = 128
 SUB = 8
 FLAT = 6
-EARLY = 12
+ETA, SUM_U, SUM_V, DEEP, PUSH_U, PUSH_V = range(FLAT)
+SOON = 4
+CHUNKS = 3
 MESH = pl.DeviceIdType.MESH
 F32 = jnp.float32
 
@@ -97,13 +99,12 @@
     tr, sr, ur, vr, tm, sm, um, vm, pm, wu, ev, xu, xv, px, huc, hvc, dz, xt, xs, yt, ys, ratio,
     zt, mt, wi, bi, de, hue, hve, flat, fu_ref, fv_ref,
     strip0, fe0, fw0, strip_a, fe_a, fw_a, strip_b, fe_b, fw_b, strip_c, fe_c,
-    strip2, fe2, fw2, mend, edge_b, acc, pn,
+    strip2, fe2, fw2, strip3, fe3, fw3, mend, edge_b, acc, pn, rim_rows,
     load_sem, send1, recv1, send2, recv2,
 ):
     levels, nt, rows, _ = t_out.shape
     end = SUB + rows
     zero = jnp.zeros((nt, SUB, LANES), F32)
-    early = EARLY * levels // 12
     nr = rows // SUB
     lon, lat = lax.axis_index("lon"), lax.axis_index("lat")
     nlon, nlat = lax.axis_size("lon"), lax.axis_size("lat")
@@ -150,7 +151,7 @@
     ld_v = load(lambda s: v_in.at[:, :, s], lambda c: vr.at[:, c, own, :])
     ld_t = load(lambda s: t_in.at[:, :, s], lambda c: tr.at[:, c, own, :])
     ld_s = load(lambda s: s_in.at[:, :, s], lambda c: sr.at[:, c, own, :])
-    ld_e = load(lambda s: eta_in.at[:, s], lambda c: flat.at[0, c, own, :])
+    ld_e = load(lambda s: eta_in.at[:, s], lambda c: flat.at[ETA, c, own, :])
     ld_z = load(lambda s: zt_in.at[:, s], lambda c: zt.at[c])
     ld_m = load(lambda s: mt_in.at[:, s], lambda c: mt.at[c])
 
@@ -162,7 +163,7 @@
     def clear(first):
         beyond = slice(first, first + SUB)
         de[:, beyond, :] = jnp.zeros((nt + 1, SUB, LANES), F32)
-        for ref in (fe0, fw0, fe_b, fw_b, fe2, fw2):
+        for ref in (fe0, fw0, fe_b, fw_b, fe2, fw2, fe3, fw3):
             ref[beyond, :] = jnp.zeros((SUB, LANES), F32)
         for f in range(FLAT):
             flat[f, :, beyond, :] = jnp.zeros((nt, SUB, LANES), F32)
@@ -337,7 +338,7 @@
     for c in along_a:
         c.start()
     arrived(ld_e, ld_z, ld_m)
-    flat[5, :, own, :] = depth
+    flat[DEEP, :, own, :] = depth
 
     def faces(first, last):
         for r in range(first, last, SUB):
@@ -415,8 +416,7 @@
             momentum(k, r, inner)
         return carry
 
-    step_loop(0, levels, 2, inside, 0)
-    step_loop(0, early, 4, east_fluxes, 0)
+    step_loop(0, levels, 3, lambda k, c: inside(k, east_fluxes(k, c)), 0)
 
     for c in along0:
         c.wait_recv()
@@ -446,23 +446,45 @@
 
     step_loop(0, levels, 6, last_sides, 0)
     step_loop(0, levels, 4, outside, 0)
+    spot8 = lax.shift_right_logical(tall, 3)
+
+    def pack(fields):
+        group = jnp.zeros((rows, LANES), F32)
+        for n, f in enumerate(fields):
+            x = jnp.where(tall < LANES // 2, flat[f, 0, own, :], flat[f, nt - 1, own, :])
+            group = jnp.where(spot8 == n, pltpu.roll(x, 8 * n + 4, 1), group)
+        return group
+
+    def far(fields, strip, fe, fw):
+        def rows_of(first):
+            return flat.at[fields, :, pl.ds(first, NSUB), :]
+
+        up = [cp2(rows_of(end - NSUB), rows_of(SUB - NSUB), lon, nth)]
+        down = [cp2(rows_of(SUB), rows_of(end), lon, sth)]
+        along, corner_up, corner_down = strips(cp2, strip, fe, fw, NSUB)
+        return along, up + corner_up, down + corner_down
+
+    cp2 = copier(send2, recv2)
+    flat[SUM_U, :, own, :] = acc[0]
+    flat[SUM_V, :, own, :] = acc[1]
+    strip3[...] = pack(range(SOON))
+    along3, up3, down3 = far(pl.ds(0, SOON), strip3, fe3, fw3)
+    for c in along3:
+        c.start()
+    start_ns(up3, down3)
+
     wind_u = jnp.where(hue[0:nt, own, :] > 0.0, (TIME_STEP * WIND_FACTOR) * zt[...], 0.0)
     wind_v = jnp.where(hve[0:nt, own, :] > 0.0, (TIME_STEP * WIND_FACTOR) * mt[...], 0.0)
     u_out[0, :, 0:rows, :] += wind_u
     v_out[0, :, 0:rows, :] += wind_v
-    flat[1, :, own, :] = acc[0]
-    flat[2, :, own, :] = acc[1]
-    flat[3, :, own, :] = acc[2] - acc[0] + wind_u
-    flat[4, :, own, :] = acc[3] - acc[1] + wind_v
+    flat[PUSH_U, :, own, :] = acc[2] - acc[0] + wind_u
+    flat[PUSH_V, :, own, :] = acc[3] - acc[1] + wind_v
 
     recv_ns(corner_up0, corner_down0)
     for out in (slice(0, SUB), slice(end, end + SUB)):
         de[nt, out, :] = pltpu.roll(jnp.where((lane & 3) >= 2, fe0[out, :], fw0[out, :]), LANES - 2, 1)
     faces(0, SUB)
     faces(end - SUB, end + SUB)
-    for c in along_b + along_c:
-        c.wait_recv()
-    recv_ns(corner_up_b, corner_down_b)
     level = lax.shift_right_logical(tall, 3).astype(F32)
 
     def by_lane(at, one, two, five, six):
@@ -472,27 +494,11 @@
         return jnp.broadcast_to(ref[c, which, at:at + 1], (n, LANES))
 
     LAST = LANES - 1
+    spot = tall & 7
     for r in range(0, end + SUB, SUB):
         here = slice(r, r + SUB)
-        limit = by_lane(lane & 7, *(column(ref, nt, at, here, SUB) for ref in (hue, hve) for at in (LAST, 0)))
-        x = jnp.where((lane & 3) >= 2, fe_b[here, :], fw_b[here, :])
-        edge_b[here, :] = jnp.where(limit > lax.shift_right_logical(lane, 3).astype(F32), x, 0.0)
-    x = edge_b[own, :]
-    spot = tall & 7
-    near = jnp.where((spot & 1) == 1, pltpu.roll(x, LAST, 1), pltpu.roll(x, 1, 1))
-    above, below = slice(SUB + 1, end + 1), slice(SUB - 1, end - 1)
-    turn_u = fu_ref[...].reshape(rows, LANES) * pltpu.roll(x + edge_b[below, :], LANES - 5, 1) - fe_c[...]
-    turn_v = fv_ref[...].reshape(rows, LANES) * pltpu.roll(x + edge_b[above, :], 5, 1)
-    extra = MIX * near + jnp.where(spot == 1, turn_u, 0.0) - jnp.where(spot == 6, turn_v, 0.0)
-    limit = by_lane(spot, column(hue, nt - 1, LAST), column(hue, 0, 0), column(hve, nt - 1, LAST), column(hve, 0, 0))
-    extra = jnp.where(limit > level, extra, 0.0)
-    total = jnp.zeros((rows, LANES), F32)
-    for k in range(levels):
-        total = total + (pltpu.roll(extra, LANES - 8 * k, 1) if k else extra)
-    total_u, total_v = pltpu.roll(total, LANES - 2, 1), pltpu.roll(total, LANES - 6, 1)
-    for f, d in ((3, total_u), (4, total_v)):
-        flat[f, 0, own, :] += jnp.where(tall == 0, d, 0.0)
-        flat[f, nt - 1, own, :] += jnp.where(tall == LAST, d, 0.0)
+        edge_b[here, :] = by_lane(lane & 7, *(column(ref, nt, at, here, SUB) for ref in (hue, hve) for at in (LAST, 0)))
+    mend[...] = by_lane(spot, column(hue, nt - 1, LAST), column(hue, 0, 0), column(hve, nt - 1, LAST), column(hve, 0, 0))
 
     recv_ns(flow_up, flow_down)
     recv_ns([], press_down)
@@ -505,45 +511,58 @@
         u = jnp.where(hue[0:nt, out, :] > kf, ur[k, :, out, :], 0.0)
         v = jnp.where(hve[0:nt, out, :] > kf, vr[k, :, out, :], 0.0)
         edge_row = slice(end - 1, end + SUB - 1)
-        du = jnp.where(top & (hue[0:nt, edge_row, :] > kf), MIX * u, 0.0)
-        dv = jnp.where(top & (hve[0:nt, edge_row, :] > kf),
+        du = jnp.where(hue[0:nt, edge_row, :] > kf, MIX * u, 0.0)
+        dv = jnp.where(hve[0:nt, edge_row, :] > kf,
                        MIX * v - fv_north * (u + west_in(u, lane)) - pn[k], 0.0)
-        row = slice(rows - 1, rows + SUB - 1)
-        u_out[k, :, row, :] += du
-        v_out[k, :, row, :] += dv
+        rim_rows[k, 0] = du
+        rim_rows[k, 1] = dv
         nu, nv = nu + du, nv + dv
 
         out = slice(SUB - 1, 2 * SUB - 1)
         u = jnp.where(hue[0:nt, out, :] > kf, ur[k, :, out, :], 0.0)
         v = jnp.where(hve[0:nt, out, :] > kf, vr[k, :, out, :], 0.0)
         edge_row = slice(SUB, 2 * SUB)
-        du = jnp.where(top & (hue[0:nt, edge_row, :] > kf),
+        du = jnp.where(hue[0:nt, edge_row, :] > kf,
                        MIX * u + fu_south * (v + east_in(v, lane, 1)), 0.0)
-        dv = jnp.where(top & (hve[0:nt, edge_row, :] > kf), MIX * v, 0.0)
-        u_out[k, :, 0:SUB, :] += du
-        v_out[k, :, 0:SUB, :] += dv
+        dv = jnp.where(hve[0:nt, edge_row, :] > kf, MIX * v, 0.0)
+        rim_rows[k, 2] = du
+        rim_rows[k, 3] = dv
         return nu, nv, su + du, sv + dv
 
     nu, nv, su, sv = step_loop(0, levels, 4, far_rows, (zero,) * 4)
-    for f, north, south in ((3, nu, su), (4, nv, sv)):
+    for f, north, south in ((PUSH_U, nu, su), (PUSH_V, nv, sv)):
+        north, south = jnp.where(top, north, 0.0), jnp.where(top, south, 0.0)
         flat[f, :, SUB:2 * SUB, :] += south
         flat[f, :, end - SUB:end, :] += pltpu.roll(north, SUB - 1, 1)
 
-    spot = lax.shift_right_logical(tall, 3)
-    group = jnp.zeros((rows, LANES), F32)
-    for f in range(FLAT):
-        x = jnp.where(tall < LANES // 2, flat[f, 0, own, :], flat[f, nt - 1, own, :])
-        group = jnp.where(spot == f, pltpu.roll(x, 8 * f + 4, 1), group)
-    strip2[...] = group
-    cp = copier(send2, recv2)
-    flat_up = [cp(cube_rows(flat, end - NSUB, NSUB), cube_rows(flat, SUB - NSUB, NSUB), lon, nth)]
-    flat_down = [cp(cube_rows(flat, SUB, NSUB), cube_rows(flat, end, NSUB), lon, sth)]
-    along2, corner_up2, corner_down2 = strips(
-        cp, strip2, fe2, fw2, NSUB)
-    start_ns(flat_up, flat_down)
+
+    for c in along_b + along_c:
+        c.wait_recv()
+    recv_ns(corner_up_b, corner_down_b)
+    for r in range(0, end + SUB, SUB):
+        here = slice(r, r + SUB)
+        x = jnp.where((lane & 3) >= 2, fe_b[here, :], fw_b[here, :])
+        edge_b[here, :] = jnp.where(edge_b[here, :] > lax.shift_right_logical(lane, 3).astype(F32), x, 0.0)
+    x = edge_b[own, :]
+    near = jnp.where((spot & 1) == 1, pltpu.roll(x, LAST, 1), pltpu.roll(x, 1, 1))
+    above, below = slice(SUB + 1, end + 1), slice(SUB - 1, end - 1)
+    turn_u = fu_ref[...].reshape(rows, LANES) * pltpu.roll(x + edge_b[below, :], LANES - 5, 1) - fe_c[...]
+    turn_v = fv_ref[...].reshape(rows, LANES) * pltpu.roll(x + edge_b[above, :], 5, 1)
+    extra = MIX * near + jnp.where(spot == 1, turn_u, 0.0) - jnp.where(spot == 6, turn_v, 0.0)
+    extra = jnp.where(mend[...] > level, extra, 0.0)
+    total = jnp.zeros((rows, LANES), F32)
+    for k in range(levels):
+        total = total + (pltpu.roll(extra, LANES - 8 * k, 1) if k else extra)
+    total_u, total_v = pltpu.roll(total, LANES - 2, 1), pltpu.roll(total, LANES - 6, 1)
+    for f, d in ((PUSH_U, total_u), (PUSH_V, total_v)):
+        flat[f, 0, own, :] += jnp.where(tall == 0, d, 0.0)
+        flat[f, nt - 1, own, :] += jnp.where(tall == LAST, d, 0.0)
+
+    strip2[...] = pack((PUSH_U, PUSH_V))
+    along2, up2, down2 = far(pl.ds(SOON, FLAT - SOON), strip2, fe2, fw2)
+    start_ns(up2, down2)
     for c in along2:
         c.start()
-    start_ns(corner_up2, corner_down2)
 
     for k in range(levels):
         du = pltpu.roll(extra, LANES - 2 - 8 * k, 1)
@@ -551,6 +570,15 @@
         for ref, d in ((u_out, du), (v_out, dv)):
             ref[k, 0, 0:rows, :] += jnp.where(tall == 0, d, 0.0)
             ref[k, nt - 1, 0:rows, :] += jnp.where(tall == LAST, d, 0.0)
+
+    def rim_updates(k, carry):
+        row = slice(rows - 1, rows + SUB - 1)
+        for n, ref in enumerate((u_out, v_out)):
+            ref[k, :, row, :] += jnp.where(top, rim_rows[k, n], 0.0)
+            ref[k, :, 0:SUB, :] += jnp.where(top, rim_rows[k, 2 + n], 0.0)
+        return carry
+
+    step_loop(0, levels, 3, rim_updates, 0)
 
     recv_ns(tracer_up, tracer_down)
 
@@ -579,7 +607,6 @@
                     - w2 * ref[k, :, a + 2:a + SUB + 2, :] + w3 * ref[k, :, a - 1:a + SUB - 1, :])
         return carry
 
-    step_loop(early, levels, 4, east_fluxes, 0)
     step_loop(0, levels, 1, north_fluxes, 0)
     for c in along_a:
         c.wait_recv()
@@ -662,25 +689,32 @@
 
         step_loop(0, levels - 1, 1, backward, (t, s))
 
-    for c in along0 + along_a + along_b + along_c:
+    count = rows + 2 * NSUB
+    wide = slice(SUB - NSUB, end + NSUB)
+    half = (lane_of((count, LANES)) & 7) >= 4
+
+    def finish(fields, fe, fw):
+        halo = jnp.where(half, fe[wide, :], fw[wide, :])
+        for n, f in enumerate(fields):
+            flat_out[f, nt, 0:count] = pltpu.roll(halo, LANES - 8 * n - 4, 1)
+            flat_out[f, 0:nt, 0:NSUB, :] = flat[f, :, SUB - NSUB:SUB, :]
+            flat_out[f, 0:nt, rows + NSUB:count, :] = flat[f, :, end:end + NSUB, :]
+
+    for f in range(FLAT):
+        flat_out[f, 0:nt, pl.ds(NSUB, rows), :] = flat[f, :, own, :]
+    flat_out[DEEP, :, count:, :] = jnp.zeros((nt + 1, SUB, LANES), F32)
+    for c in along3:
+        c.wait_recv()
+    recv_ns(up3, down3)
+    finish(range(SOON), fe3, fw3)
+    for c in along0 + along_a + along_b + along_c + along2 + along3:
         c.wait_send()
-    sent_ns(depth_up + corner_up0 + flow_up + tracer_up + corner_up_b,
-            depth_down + corner_down0 + flow_down + tracer_down + corner_down_b + press_down)
-    recv_ns(flat_up, flat_down)
+    sent_ns(depth_up + corner_up0 + flow_up + tracer_up + corner_up_b + up2 + up3,
+            depth_down + corner_down0 + flow_down + tracer_down + corner_down_b + press_down + down2 + down3)
     for c in along2:
         c.wait_recv()
-    recv_ns(corner_up2, corner_down2)
-    wide = slice(SUB - NSUB, end + NSUB)
-    count = rows + 2 * NSUB
-    halo = jnp.where((lane_of((count, LANES)) & 7) >= 4, fe2[wide, :], fw2[wide, :])
-    for f in range(FLAT):
-        flat_out[f, 0:nt, 0:count] = flat[f, :, wide, :]
-        flat_out[f, nt, 0:count] = pltpu.roll(halo, LANES - 8 * f - 4, 1)
-    flat_out[5, :, count:, :] = jnp.zeros((nt + 1, SUB, LANES), F32)
-
-    for c in along2:
-        c.wait_send()
-    sent_ns(flat_up + corner_up2, flat_down + corner_down2)
+    recv_ns(up2, down2)
+    finish((PUSH_U, PUSH_V), fe2, fw2)
 
 
 def tail(
@@ -706,13 +740,13 @@
         ref[:, 0:SUB, :] = jnp.zeros((nt + 1, SUB, LANES), F32)
         ref[:, count + SUB:, :] = jnp.zeros((nt + 1, SUB, LANES), F32)
     tiles = range(0, count, SUB)
-    eta[:, SUB:count + SUB, :] = flat[0, :, 0:count, :]
-    bu[:, SUB:count + SUB, :] = flat[1, :, 0:count, :]
-    bv[:, SUB:count + SUB, :] = flat[2, :, 0:count, :]
+    eta[:, SUB:count + SUB, :] = flat[ETA, :, 0:count, :]
+    bu[:, SUB:count + SUB, :] = flat[SUM_U, :, 0:count, :]
+    bv[:, SUB:count + SUB, :] = flat[SUM_V, :, 0:count, :]
     for r in tiles:
-        d = flat[5, :, r:r + SUB, :]
+        d = flat[DEEP, :, r:r + SUB, :]
         hx[:, r:r + SUB, :] = jnp.minimum(d, east_all(d, lane))
-        hy[:, r:r + SUB, :] = jnp.minimum(d, flat[5, :, r + 1:r + SUB + 1, :])
+        hy[:, r:r + SUB, :] = jnp.minimum(d, flat[DEEP, :, r + 1:r + SUB + 1, :])
     for sub in range(NSUB):
         for r in tiles:
             here, below = slice(SUB + r, 2 * SUB + r), slice(SUB + r - 1, 2 * SUB + r - 1)
@@ -723,9 +757,9 @@
             here, above = slice(SUB + r, 2 * SUB + r), slice(SUB + r + 1, 2 * SUB + r + 1)
             raw = slice(r, r + SUB)
             x = eta[:, here, :]
-            bu[:, here, :] = (bu[:, here, :] + (1.0 / NSUB) * flat[3, :, raw, :]
+            bu[:, here, :] = (bu[:, here, :] + (1.0 / NSUB) * flat[PUSH_U, :, raw, :]
                               - SLOPE_FACTOR * hx[:, raw, :] * (east_all(x, lane) - x))
-            bv[:, here, :] = (bv[:, here, :] + (1.0 / NSUB) * flat[4, :, raw, :]
+            bv[:, here, :] = (bv[:, here, :] + (1.0 / NSUB) * flat[PUSH_V, :, raw, :]
                               - SLOPE_FACTOR * hy[:, raw, :] * (eta[:, above, :] - x))
     mid = pl.ds(SUB + NSUB, rows)
     put(lambda c: eta.at[c, mid, :], lambda d: eta_out.at[:, d])
@@ -737,19 +771,24 @@
         hu, hv = hx[0:nt, raw, :], hy[0:nt, raw, :]
         done = slice(SUB + NSUB + r, 2 * SUB + NSUB + r)
         out = slice(r, r + SUB)
-        cor[0, :, out, :] = (bu[0:nt, done, :] - (flat[3, 0:nt, raw, :] + flat[1, 0:nt, raw, :])) / jnp.maximum(hu, 1.0)
-        cor[1, :, out, :] = (bv[0:nt, done, :] - (flat[4, 0:nt, raw, :] + flat[2, 0:nt, raw, :])) / jnp.maximum(hv, 1.0)
+        cor[0, :, out, :] = (bu[0:nt, done, :] - (flat[PUSH_U, 0:nt, raw, :] + flat[SUM_U, 0:nt, raw, :])) / jnp.maximum(hu, 1.0)
+        cor[1, :, out, :] = (bv[0:nt, done, :] - (flat[PUSH_V, 0:nt, raw, :] + flat[SUM_V, 0:nt, raw, :])) / jnp.maximum(hv, 1.0)
         cor[2, :, out, :] = hu
         cor[3, :, out, :] = hv
 
-    @pl.loop(0, levels)
-    def _(k):
-        kf = k.astype(F32)
-        un[k] = jnp.where(cor[2] > kf, ut[k, :, 0:rows, :] + cor[0], 0.0)
-        vn[k] = jnp.where(cor[3] > kf, vt[k, :, 0:rows, :] + cor[1], 0.0)
-
-    put(lambda c: un.at[:, c], lambda d: u_out.at[:, :, d])
-    put(lambda c: vn.at[:, c], lambda d: v_out.at[:, :, d])
+    part = -(-levels // CHUNKS)
+    for first in range(0, levels, part):
+        last = min(first + part, levels)
+
+        @pl.loop(first, last)
+        def _(k):
+            kf = k.astype(F32)
+            un[k] = jnp.where(cor[2] > kf, ut[k, :, 0:rows, :] + cor[0], 0.0)
+            vn[k] = jnp.where(cor[3] > kf, vt[k, :, 0:rows, :] + cor[1], 0.0)
+
+        span = pl.ds(first, last - first)
+        put(lambda c: un.at[span, c], lambda d: u_out.at[span, :, d])
+        put(lambda c: vn.at[span, c], lambda d: v_out.at[span, :, d])
     for c in copies:
         c.wait()
 
@@ -771,7 +810,7 @@
     raw = vmem(levels, nt, erows, LANES)
     own = vmem(levels, nt, rows, LANES)
     ints = pltpu.VMEM((nt, rows, LANES), jnp.int32)
-    n1, n2 = 2 + 8 + 1 + 6 + 4 + 3, 2 + 6
+    n1, n2 = 2 + 8 + 1 + 6 + 4 + 3, 2 * (2 + 6)
     cube = (levels, nt, rows, LANES)
     parts = pl.pallas_call(
         functools.partial(kernel, rows * lax.axis_size("lat")),
@@ -789,8 +828,10 @@
             + [vmem(rows, LANES)] * 3
             + [vmem(rows, LANES), vmem(erows, LANES), vmem(erows, LANES)]
             + [vmem(rows, LANES)] * 2
-            + [vmem(rows, LANES), vmem(erows, LANES), vmem(erows, LANES), vmem(rows, LANES)]
-            + [vmem(erows, LANES), vmem(4, nt, rows, LANES), vmem(levels, nt, SUB, LANES)]
+            + [vmem(rows, LANES), vmem(erows, LANES), vmem(erows, LANES)] * 2
+            + [vmem(rows, LANES)]
+            + [vmem(erows, LANES), vmem(4, nt, rows, LANES), vmem(levels, nt, SUB, LANES),
+               vmem(levels, 4, nt, SUB, LANES)]
             + [pltpu.SemaphoreType.DMA((9 * nt,))]
             + [pltpu.SemaphoreType.DMA((n1,))] * 2
             + [pltpu.SemaphoreType.DMA((n2,))] * 2
@@ -807,7 +848,7 @@
         scratch_shapes=(
             [vmem(nt + 1, count + 2 * SUB, LANES)] * 3 + [vmem(nt + 1, count, LANES)] * 2
             + [own, own, vmem(4, nt, rows, LANES)]
-            + [pltpu.SemaphoreType.DMA((7 * nt,))]
+            + [pltpu.SemaphoreType.DMA(((5 + 2 * CHUNKS) * nt,))]
         ),
         compiler_params=pltpu.CompilerParams(vmem_limit_bytes=32 * 1024 * 1024),
     )(*parts)

time: 17.2 us -> 17 us (0.988)
  Pallas kernels: 16.4 us -> 16.2 us
where the time goes in v6:
time: 17 us; the launch traced here: 16.9 us
  Pallas kernels  16.2 us (95%)
  between operations  0.64 us (4%)
    pallas_call x1, Pallas kernels, body(): pl.pallas_call(functools.partial(kernel, rows * lax.axis_size('lat')), ou...  14.2 us
    pallas_call x1, Pallas kernels, body(): pl.pallas_call(tail, out_shape=(pltpu.HBM(cube, F32),) * 4 + (pltpu.HBM(p...  2.03 us

profile of v6, /device:TPU:0, one launch (start us, length us, event | category | flops | bytes accessed | tf_op | source)
XLA Modules:
  0.0 16.9 jit_solution(6547273043397760512)
XLA Ops:
  0.6 14.2 %shard_map.144 = (f32[12,3,32,128]{3,2,1,0:T(8,128)S(1)}, f32[12,3,32,128]{3,2,1,0:T(8,128)S(1)}, f32[12,3,40,128]{3,2,1,0:T(8,128)S(1)}, f32[12,3,40,128]{3,2,1,0:T(8,128)S(1)}, f32[6,4,48,128]{3,2,1,0:T(8,128)S(1)}) custom-call(f32[12,32,384]{2,1,0:T(8,128)} %t_in.1, f32[12,32,384]{2,1,0:T(8,128)} %s_in.1, f32[12,32,384]{2,1,0:T(8,128)} %u_in.1, ...), custom_call_target="tpu_custom_call" | custom-call | tf_op jit(solution)/shard_map/pallas_call | solution.py:815
  14.9 2.0 %shard_map.145 = (f32[12,32,384]{2,1,0:T(8,128)}, f32[12,32,384]{2,1,0:T(8,128)}, f32[12,32,384]{2,1,0:T(8,128)}, f32[12,32,384]{2,1,0:T(8,128)}, f32[32,384]{1,...) custom-call(f32[12,3,32,128]{3,2,1,0:T(8,128)S(1)} %get-tuple-element.12.t, ...), custom_call_target="tpu_custom_call" | custom-call | tf_op jit(solution)/shard_map/pallas_call | solution.py:843

commit v7 on v6

--- a/solution.py
+++ b/solution.py
@@ -444,8 +444,8 @@
         momentum(k, nr - 1, slice(0, nt))
         return carry
 
-    step_loop(0, levels, 6, last_sides, 0)
-    step_loop(0, levels, 4, outside, 0)
+    step_loop(0, levels, levels, last_sides, 0)
+    step_loop(0, levels, levels, outside, 0)
     spot8 = lax.shift_right_logical(tall, 3)
 
     def pack(fields):
@@ -529,7 +529,7 @@
         rim_rows[k, 3] = dv
         return nu, nv, su + du, sv + dv
 
-    nu, nv, su, sv = step_loop(0, levels, 4, far_rows, (zero,) * 4)
+    nu, nv, su, sv = step_loop(0, levels, levels, far_rows, (zero,) * 4)
     for f, north, south in ((PUSH_U, nu, su), (PUSH_V, nv, sv)):
         north, south = jnp.where(top, north, 0.0), jnp.where(top, south, 0.0)
         flat[f, :, SUB:2 * SUB, :] += south

time: 17 us -> 16.6 us (0.976)
  Pallas kernels: 16.2 us -> 15.8 us
    pallas_call x1, Pallas kernels: 14.2 us -> 13.8 us  [body(): pl.pallas_call(functools.partial(kernel, rows * lax.axis_size('lat')), ou...]
where the time goes in v7:
time: 16.6 us; the launch traced here: 16.4 us
  Pallas kernels  15.8 us (95%)
  between operations  0.64 us (4%)
    pallas_call x1, Pallas kernels, body(): pl.pallas_call(functools.partial(kernel, rows * lax.axis_size('lat')), ou...  13.8 us
    pallas_call x1, Pallas kernels, body(): pl.pallas_call(tail, out_shape=(pltpu.HBM(cube, F32),) * 4 + (pltpu.HBM(p...  2.03 us

profile of v7, /device:TPU:0, one launch (start us, length us, event | category | flops | bytes accessed | tf_op | source)
XLA Modules:
  0.0 16.4 jit_solution(17703222487023321244)
XLA Ops:
  0.6 13.8 %shard_map.144 = (f32[12,3,32,128]{3,2,1,0:T(8,128)S(1)}, f32[12,3,32,128]{3,2,1,0:T(8,128)S(1)}, f32[12,3,40,128]{3,2,1,0:T(8,128)S(1)}, f32[12,3,40,128]{3,2,1,0:T(8,128)S(1)}, f32[6,4,48,128]{3,2,1,0:T(8,128)S(1)}) custom-call(f32[12,32,384]{2,1,0:T(8,128)} %t_in.1, f32[12,32,384]{2,1,0:T(8,128)} %s_in.1, f32[12,32,384]{2,1,0:T(8,128)} %u_in.1, ...), custom_call_target="tpu_custom_call" | custom-call | tf_op jit(solution)/shard_map/pallas_call | solution.py:815
  14.4 2.0 %shard_map.145 = (f32[12,32,384]{2,1,0:T(8,128)}, f32[12,32,384]{2,1,0:T(8,128)}, f32[12,32,384]{2,1,0:T(8,128)}, f32[12,32,384]{2,1,0:T(8,128)}, f32[32,384]{1,...) custom-call(f32[12,3,32,128]{3,2,1,0:T(8,128)S(1)} %get-tuple-element.12.t, ...), custom_call_target="tpu_custom_call" | custom-call | tf_op jit(solution)/shard_map/pallas_call | solution.py:843
